TPU v7x, 512 devices: a whole 4x8x8 slice. The times are simulated.
512 devices in a mesh: gx: 16 (over y, core), gy: 32 (over z, x).
Axes of the slice: x: 4, y: 8, z: 8, core: 2. Of those that a mesh axis runs over, the one named last changes fastest.
Arguments:
- query_rows: bfloat16 [65536, 1024], P(('gx', 'gy')), may hold values from -6 to 6
- key_rows: bfloat16 [65536, 1024], P(('gx', 'gy')), may hold values from -6 to 6
- value_rows: bfloat16 [65536, 1024], P(('gx', 'gy')), may hold values from -6 to 6
- out_grad: bfloat16 [65536, 1024], P(('gx', 'gy')), may hold values from -6 to 6
- gate_class: int32 [65536], P(('gx', 'gy')), may hold values from 0 to 31
- gate_table: float32 [32, 20, 8], replicated, may hold values from 0 to 1, as said below
Outputs:
- query_grad: bfloat16 [65536, 1024], P(('gx', 'gy'))
- key_grad: bfloat16 [65536, 1024], P(('gx', 'gy'))
- value_grad: bfloat16 [65536, 1024], P(('gx', 'gy'))
Inputs may be any that keep to these rules, and one draw needn't show every extreme that they name: `gate_class`: row of the gate table for each token. `gate_table`: every entry is positive.
All inputs are finite; a program needn't handle non-finite values.
Results may differ from a plain program's by a relative error of at most 0.0054.
Values may be sent and summed in bfloat16 or wider, within the bound.
A program may use at most 64 MiB of HBM per device.

v0:
```python
import jax
import jax.numpy as jnp
from jax import lax
from jax.sharding import PartitionSpec as P


def from_partner(block, axis, stride):
    count = lax.axis_size(axis)
    route = []
    for low in range(count):
        high = low | 1 << stride
        if high != low and high < count:
            route += [(low, high), (high, low)]
    return lax.ppermute(block, axis, route)


def level_bits(amount):
    return amount.bit_length() - 1


def gate_values(gate_class, gate_table):
    classes = gate_table.shape[0]
    levels = gate_table.shape[1]
    head_count = gate_table.shape[2]
    picker = (gate_class[:, None] == jnp.arange(classes, dtype=jnp.int32)[None, :]).astype(
        jnp.float32
    )
    flat_table = gate_table.reshape(classes, levels * head_count)
    picked = jnp.dot(
        picker, flat_table, precision=lax.Precision.HIGHEST, preferred_element_type=jnp.float32
    )
    return picked.reshape(gate_class.shape[0], levels, head_count)


def block_weights(gate_rows, amount):
    block_depth = level_bits(amount)
    positions = jnp.arange(amount, dtype=jnp.int32)
    xor_place = jnp.bitwise_xor(positions[:, None], positions[None, :])
    level_map = jnp.zeros((amount, amount), jnp.int32)
    for bit_index in range(block_depth):
        level_map = level_map + (xor_place >= 2**bit_index).astype(jnp.int32)
    causal = positions[None, :] <= positions[:, None]
    weights = jnp.zeros((gate_rows.shape[2], amount, amount), jnp.float32)
    for tree_level in range(block_depth + 1):
        chosen = jnp.logical_and(level_map == tree_level, causal)
        picked = gate_rows[:, tree_level, :].T[:, :, None]
        weights = weights + jnp.where(chosen[None, :, :], picked, jnp.zeros((), jnp.float32))
    return weights


def per_device(query_rows, key_rows, value_rows, out_grad, gate_class, gate_table):
    row_count = query_rows.shape[0]
    head_count = gate_table.shape[2]
    head_size = query_rows.shape[1] // head_count
    inner_bits = level_bits(lax.axis_size("gy"))
    outer_bits = level_bits(lax.axis_size("gx"))
    total_levels = inner_bits + outer_bits
    block_depth = level_bits(row_count)
    inner_index = lax.axis_index("gy")
    outer_index = lax.axis_index("gx")
    flag_list = [inner_index // 2**tree_level % 2 for tree_level in range(inner_bits)]
    flag_list = flag_list + [outer_index // 2**tree_level % 2 for tree_level in range(outer_bits)]
    bit_flags = jnp.stack(flag_list).astype(jnp.float32)
    gate_rows = gate_values(gate_class, gate_table)
    device_gates = (
        gate_rows[:, block_depth + 1 : block_depth + 1 + total_levels, :] * bit_flags[None, :, None]
    )
    query_heads = query_rows.reshape(row_count, head_count, head_size)
    key_heads = key_rows.reshape(row_count, head_count, head_size)
    value_heads = value_rows.reshape(row_count, head_count, head_size)
    grad_heads = out_grad.reshape(row_count, head_count, head_size)
    scores = jnp.einsum("thd,shd->hts", query_heads, key_heads, preferred_element_type=jnp.float32)
    pair_grads = jnp.einsum(
        "the,she->hts", grad_heads, value_heads, preferred_element_type=jnp.float32
    )
    weights = block_weights(gate_rows, row_count)
    weighted_grads = (weights * pair_grads).astype(jnp.bfloat16)
    weighted_scores = (weights * scores).astype(jnp.bfloat16)
    query_total = jnp.einsum(
        "hts,shd->thd", weighted_grads, key_heads, preferred_element_type=jnp.float32
    )
    key_total = jnp.einsum(
        "hts,thd->shd", weighted_grads, query_heads, preferred_element_type=jnp.float32
    )
    value_total = jnp.einsum(
        "hts,the->she", weighted_scores, grad_heads, preferred_element_type=jnp.float32
    )
    group_state = jnp.einsum(
        "thd,the->hde", key_heads, value_heads, preferred_element_type=jnp.float32
    )
    scaled_query = (device_gates[:, :, :, None] * query_heads[:, None, :, :]).astype(jnp.bfloat16)
    level_grads = jnp.einsum(
        "tlhd,the->lhde", scaled_query, grad_heads, preferred_element_type=jnp.float32
    )
    acc_state = group_state
    inner_grads = [level_grads[tree_level] for tree_level in range(inner_bits)]
    state_grad = jnp.zeros_like(group_state)
    rounded_states = []
    for tree_level in range(inner_bits):
        bundle = jnp.stack([acc_state] + inner_grads[tree_level:])
        arrived = from_partner(bundle, "gy", tree_level)
        rounded_states.append(arrived[0].astype(jnp.bfloat16))
        state_grad = state_grad + arrived[1]
        acc_state = acc_state + arrived[0]
        for later in range(tree_level + 1, inner_bits):
            inner_grads[later] = inner_grads[later] + arrived[1 + later - tree_level]
    flat_rows = head_count * head_size
    share_rows = flat_rows // lax.axis_size("gy")
    row_state = acc_state.reshape(flat_rows, head_size)
    state_share = lax.dynamic_slice_in_dim(row_state, inner_index * share_rows, share_rows, 0)
    outer_flat = level_grads[inner_bits:].reshape(outer_bits, flat_rows, head_size)
    grad_share = lax.psum_scatter(outer_flat, "gy", scatter_dimension=1, tiled=True)
    share_grads = [grad_share[tree_level] for tree_level in range(outer_bits)]
    share_total = jnp.zeros_like(state_share)
    state_parts = []
    for tree_level in range(outer_bits):
        bundle = jnp.stack([state_share] + share_grads[tree_level:])
        arrived = from_partner(bundle, "gx", tree_level)
        state_parts.append(arrived[0])
        share_total = share_total + arrived[1]
        state_share = state_share + arrived[0]
        for later in range(tree_level + 1, outer_bits):
            share_grads[later] = share_grads[later] + arrived[1 + later - tree_level]
    part_stack = jnp.stack(state_parts)
    state_rows = lax.all_gather(part_stack.astype(jnp.bfloat16), "gy", axis=1, tiled=True)
    for tree_level in range(outer_bits):
        rounded_states.append(state_rows[tree_level].reshape(head_count, head_size, head_size))
    grad_rows = lax.all_gather(share_total, "gy", axis=0, tiled=True)
    state_grad = state_grad + grad_rows.reshape(head_count, head_size, head_size)
    for tree_level in range(total_levels):
        level_term = jnp.einsum(
            "the,hde->thd",
            grad_heads,
            rounded_states[tree_level],
            preferred_element_type=jnp.float32,
        )
        query_total = query_total + device_gates[:, tree_level, :, None] * level_term
    grad_rounded = state_grad.astype(jnp.bfloat16)
    key_total = key_total + jnp.einsum(
        "the,hde->thd", value_heads, grad_rounded, preferred_element_type=jnp.float32
    )
    value_total = value_total + jnp.einsum(
        "thd,hde->the", key_heads, grad_rounded, preferred_element_type=jnp.float32
    )
    width = head_count * head_size
    return (
        query_total.reshape(row_count, width).astype(jnp.bfloat16),
        key_total.reshape(row_count, width).astype(jnp.bfloat16),
        value_total.reshape(row_count, width).astype(jnp.bfloat16),
    )


def solution(mesh):
    return jax.shard_map(
        per_device,
        mesh=mesh,
        in_specs=(
            P(("gx", "gy"), None),
            P(("gx", "gy"), None),
            P(("gx", "gy"), None),
            P(("gx", "gy"), None),
            P(("gx", "gy")),
            P(),
        ),
        out_specs=(P(("gx", "gy"), None), P(("gx", "gy"), None), P(("gx", "gy"), None)),
        check_vma=False,
    )
```

profile of v0, /device:TPU:1, one launch (start us, length us, event | category | flops | bytes accessed | tf_op | source)
XLA Modules:
  0.0 556.3 jit_solution(18360754369471738012)
XLA Ops:
  7.4 0.1 stack.115
  7.5 1.0 copy.68
  8.6 0.2 copy.40
  8.8 0.2 fusion.105
  9.1 0.8 fusion.2
  9.9 0.3 slice.282
  10.2 0.6 copy-done.3
  10.9 0.3 fusion.54
  11.2 0.3 pad_maximum_fusion
  11.5 3.9 collective-permute-start
  15.5 62.9 %collective-permute-done = f32[6,8,128,128]{3,2,1,0:T(8,128)S(1)} collective-permute-done((f32[6,8,128,128]{3,2,1,0:T(8,128)S(1)}, f32[6,8,128,128]{3,2,1,0:T(8,128)S(1)}, u32[]{:S(2)}, u32[]{:S(2)}) %collective-permute-start) | collective-permute-done | bytes 3145760 | tf_op jit(solution)/shard_map/ppermute | solution.py:14
  78.7 9.5 %collective-permute-start.1 = (f32[5,8,128,128]{3,2,1,0:T(8,128)S(1)}, f32[5,8,128,128]{3,2,1,0:T(8,128)S(1)}, u32[]{:S(2)}, u32[]{:S(2)}) collective-permute-start(f32[5,8,128,128]{3,2,1,0:T(8,128)S(1)} %fusion.99), channel_id=1, source_target_pairs={{0,2},{2,0},{1,3},{3,1},{4,6},{6,4},{5,7},{7,5},{8,10},{10,8},{9,1... | collective-permute-start | bytes 7864328 | tf_op jit(solution)/shard_map/ppermute | solution.py:14
  88.2 55.4 %collective-permute-done.1 = f32[5,8,128,128]{3,2,1,0:T(8,128)S(1)} collective-permute-done((f32[5,8,128,128]{3,2,1,0:T(8,128)S(1)}, f32[5,8,128,128]{3,2,1,0:T(8,128)S(1)}, u32[]{:S(2)}, u32[]{:S(2)}) %collective-permute-start.1) | collective-permute-done | bytes 2621472 | tf_op jit(solution)/shard_map/ppermute | solution.py:14
  143.6 0.3 slice_add_fusion.9
  144.0 1.1 copy-done.2
  145.1 0.1 fusion.93
  145.2 1.5 pad_maximum_fusion.1
  146.7 4.2 collective-permute-start.2
  150.9 1.5 slice.307
  152.5 44.6 %collective-permute-done.2 = f32[4,8,128,128]{3,2,1,0:T(8,128)} collective-permute-done((f32[4,8,128,128]{3,2,1,0:T(8,128)}, f32[4,8,128,128]{3,2,1,0:T(8,128)}, u32[]{:S(2)}, u32[]{:S(2)}) %collective-permute-start.2) | collective-permute-done | bytes 2097184 | tf_op jit(solution)/shard_map/ppermute | solution.py:14
  197.1 1.5 fusion.38
  198.6 1.3 slice_add_fusion.6
  199.9 0.1 pad_maximum_fusion.2
  200.1 6.1 %collective-permute-start.3 = (f32[3,8,128,128]{3,2,1,0:T(8,128)S(1)}, f32[3,8,128,128]{3,2,1,0:T(8,128)S(1)}, u32[]{:S(2)}, u32[]{:S(2)}) collective-permute-start(f32[3,8,128,128]{3,2,1,0:T(8,128)S(1)} %pad_maximum_fusion.2), channel_id=1, source_target_pairs={{0,8},{8,0},{1,9},{9,1},{2,10},{10,2},{3,11},{11,3},{4,12},{12,4},... | collective-permute-start | bytes 4718600 | tf_op jit(solution)/shard_map/ppermute | solution.py:14
  206.2 71.9 %collective-permute-done.3 = f32[3,8,128,128]{3,2,1,0:T(8,128)S(1)} collective-permute-done((f32[3,8,128,128]{3,2,1,0:T(8,128)S(1)}, f32[3,8,128,128]{3,2,1,0:T(8,128)S(1)}, u32[]{:S(2)}, u32[]{:S(2)}) %collective-permute-start.3) | collective-permute-done | bytes 1572896 | tf_op jit(solution)/shard_map/ppermute | solution.py:14
  278.2 1.1 pad_maximum_fusion.3
  279.3 8.7 %collective-permute-start.4 = (f32[2,8,128,128]{3,2,1,0:T(8,128)}, f32[2,8,128,128]{3,2,1,0:T(8,128)}, u32[]{:S(2)}, u32[]{:S(2)}) collective-permute-start(f32[2,8,128,128]{3,2,1,0:T(8,128)} %pad_maximum_fusion.3), channel_id=1, source_target_pairs={{0,16},{16,0},{1,17},{17,1},{2,18},{18,2},{3,19},{19,3},{4,20},{20... | collective-permute-start | bytes 3145736 | tf_op jit(solution)/shard_map/ppermute | solution.py:14
  288.3 2.2 convolution_bitcast_fusion
  290.6 43.6 %collective-permute-done.4 = f32[2,8,128,128]{3,2,1,0:T(8,128)} collective-permute-done((f32[2,8,128,128]{3,2,1,0:T(8,128)}, f32[2,8,128,128]{3,2,1,0:T(8,128)}, u32[]{:S(2)}, u32[]{:S(2)}) %collective-permute-start.4) | collective-permute-done | bytes 1048608 | tf_op jit(solution)/shard_map/ppermute | solution.py:14
  334.1 1.1 fusion.42
  335.3 0.8 copy-done.11
  336.0 102.9 %reduce-scatter.2.cloned.1.call-done = f32[4,32,128]{2,1,0:T(8,128)} async-done(((f32[4,1024,128]{2,1,0:T(8,128)}), f32[4,32,128]{2,1,0:T(8,128)}) %reduce-scatter.2.cloned.1.call-update) | async-done | bytes 65552 | tf_op jit(solution)/shard_map/reduce_scatter | solution.py:112
  438.9 0.9 pad_maximum_fusion.4
  439.8 8.0 %collective-permute-start.5 = (f32[5,32,128]{2,1,0:T(8,128)S(1)}, f32[5,32,128]{2,1,0:T(8,128)S(1)}, u32[]{:S(2)}, u32[]{:S(2)}) collective-permute-start(f32[5,32,128]{2,1,0:T(8,128)S(1)} %pad_maximum_fusion.4), channel_id=1, source_target_pairs={{0,32},{32,0},{64,96},{96,64},{128,160},{160,128},{192,224},{224,1... | collective-permute-start | bytes 245768 | tf_op jit(solution)/shard_map/ppermute | solution.py:14
  447.8 1.4 fusion.26
  449.3 0.7 bitcast_add_fusion.2
  450.0 3.2 collective-permute-start.6
  453.2 1.1 convolution_bitcast_fusion.1
  454.3 1.3 collective-permute-done.6
  455.6 4.1 collective-permute-start.7
  459.6 0.3 convolution_bitcast_fusion.13
  460.0 1.3 collective-permute-done.7
  461.3 7.6 %collective-permute-start.8 = (f32[2,32,128]{2,1,0:T(8,128)S(1)}, f32[2,32,128]{2,1,0:T(8,128)S(1)}, u32[]{:S(2)}, u32[]{:S(2)}) collective-permute-start(f32[2,32,128]{2,1,0:T(8,128)S(1)} %pad_maximum_fusion.7), channel_id=1, source_target_pairs={{0,256},{256,0},{32,288},{288,32},{64,320},{320,64},{96,352},{352,... | collective-permute-start | bytes 98312 | tf_op jit(solution)/shard_map/ppermute | solution.py:14
  469.1 1.3 collective-permute-done.8
  470.4 0.6 pad_maximum_fusion.8
  471.0 2.2 fusion.15
  473.2 2.1 fusion.16
  475.3 1.1 fusion.17
  476.4 2.2 fusion.18
  478.6 36.5 %all-gather = f32[1,1024,128]{2,1,0:T(8,128)S(1)} all-gather(f32[1,32,128]{2,1,0:T(8,128)S(1)} %slice_add_fusion.14), channel_id=2, replica_groups=mesh['gx'=16,'gy'=32] {'gy'}, dimensions={1}, use_global_device_ids=true | all-gather | bytes 540672 | tf_op jit(solution)/shard_map/all_gather | solution.py:128
  515.0 1.7 fusion.32
  516.8 0.3 fusion.29
  517.1 0.9 copy.58
  517.9 1.4 fusion.28
  519.3 0.9 copy.59
  520.2 24.2 %all-gather.3.cloned.1.call-done = bf16[4,1024,128]{2,1,0:T(8,128)(2,1)} async-done(((bf16[4,32,128]{2,1,0:T(8,128)(2,1)}), bf16[4,1024,128]{2,1,0:T(8,128)(2,1)}) %all-gather.3.cloned.1.call-update) | async-done | bytes 1048592 | tf_op jit(solution)/shard_map/all_gather | solution.py:125
  544.3 1.3 fusion.140
  545.6 0.3 fusion.22
  545.9 0.3 fusion.19
  546.2 0.3 fusion.21
  546.5 0.3 fusion.20
  546.9 0.2 copy-done.7
  547.1 1.5 fusion.25
  548.6 0.9 copy.57
  (61 shorter events, 1.3 us)
Async XLA Ops:
  7.2 1.9 copy-start
  7.2 1.6 copy-start.13
  7.2 1.6 copy-start.14
  7.2 431.7 %reduce-scatter.2.cloned.1.call-start = ((), (), s32[]{:S(2)}) async-start(), calls=%async_computation.1 | async-start | bytes 2162688 | tf_op jit(solution)/shard_map/reduce_scatter | solution.py:112
  9.9 1.0 copy-start.3
  9.9 1.0 copy-start.9
  11.5 66.8 %collective-permute-start = (f32[6,8,128,128]{3,2,1,0:T(8,128)S(1)}, f32[6,8,128,128]{3,2,1,0:T(8,128)S(1)}, u32[]{:S(2)}, u32[]{:S(2)}) collective-permute-start(f32[6,8,128,128]{3,2,1,0:T(8,128)S(1)} %pad_maximum_fusion), channel_id=1, source_target_pairs={{0,1},{1,0},{2,3},{3,2},{4,5},{5,4},{6,7},{7,6},{8,9},{9,8},{10,11... | collective-permute-start | bytes 9437192 | tf_op jit(solution)/shard_map/ppermute | solution.py:14
  78.4 65.6 %copy-start.1 = (f32[6,8,128,128]{3,2,1,0:T(8,128)}, f32[6,8,128,128]{3,2,1,0:T(8,128)S(1)}, u32[]{:S(2)}) copy-start(f32[6,8,128,128]{3,2,1,0:T(8,128)S(1)} %collective-permute-done) | copy-start | bytes 9437188
  78.7 64.9 %collective-permute-start.1 = (f32[5,8,128,128]{3,2,1,0:T(8,128)S(1)}, f32[5,8,128,128]{3,2,1,0:T(8,128)S(1)}, u32[]{:S(2)}, u32[]{:S(2)}) collective-permute-start(f32[5,8,128,128]{3,2,1,0:T(8,128)S(1)} %fusion.99), channel_id=1, source_target_pairs={{0,2},{2,0},{1,3},{3,1},{4,6},{6,4},{5,7},{7,5},{8,10},{10,8},{9,1... | collective-permute-start | bytes 7864328 | tf_op jit(solution)/shard_map/ppermute | solution.py:14
  143.6 1.5 copy-start.2
  146.7 50.4 %collective-permute-start.2 = (f32[4,8,128,128]{3,2,1,0:T(8,128)}, f32[4,8,128,128]{3,2,1,0:T(8,128)}, u32[]{:S(2)}, u32[]{:S(2)}) collective-permute-start(f32[4,8,128,128]{3,2,1,0:T(8,128)} %pad_maximum_fusion.1), channel_id=1, source_target_pairs={{0,4},{4,0},{1,5},{5,1},{2,6},{6,2},{3,7},{7,3},{8,12},{12,8},{9,1... | collective-permute-start | bytes 6291464 | tf_op jit(solution)/shard_map/ppermute | solution.py:14
  152.5 391.9 %all-gather.3.cloned.1.call-start = ((), (), s32[]{:S(2)}) async-start(), calls=%async_computation.2 | async-start | bytes 1081344 | tf_op jit(solution)/shard_map/all_gather | solution.py:125
  200.1 88.3 %copy-start.10 = (bf16[128,1024]{1,0:T(8,128)(2,1)S(1)}, bf16[128,1024]{1,0:T(8,128)(2,1)}, u32[]{:S(2)}) copy-start(bf16[128,1024]{1,0:T(8,128)(2,1)} %param.6) | copy-start | bytes 786436
  200.1 78.0 %collective-permute-start.3 = (f32[3,8,128,128]{3,2,1,0:T(8,128)S(1)}, f32[3,8,128,128]{3,2,1,0:T(8,128)S(1)}, u32[]{:S(2)}, u32[]{:S(2)}) collective-permute-start(f32[3,8,128,128]{3,2,1,0:T(8,128)S(1)} %pad_maximum_fusion.2), channel_id=1, source_target_pairs={{0,8},{8,0},{1,9},{9,1},{2,10},{10,2},{3,11},{11,3},{4,12},{12,4},... | collective-permute-start | bytes 4718600 | tf_op jit(solution)/shard_map/ppermute | solution.py:14
  279.3 54.9 %collective-permute-start.4 = (f32[2,8,128,128]{3,2,1,0:T(8,128)}, f32[2,8,128,128]{3,2,1,0:T(8,128)}, u32[]{:S(2)}, u32[]{:S(2)}) collective-permute-start(f32[2,8,128,128]{3,2,1,0:T(8,128)} %pad_maximum_fusion.3), channel_id=1, source_target_pairs={{0,16},{16,0},{1,17},{17,1},{2,18},{18,2},{3,19},{19,3},{4,20},{20... | collective-permute-start | bytes 3145736 | tf_op jit(solution)/shard_map/ppermute | solution.py:14
  335.3 0.8 copy-start.11
  438.9 11.1 %copy-start.12 = (f32[4,32,128]{2,1,0:T(8,128)S(1)}, f32[4,32,128]{2,1,0:T(8,128)}, u32[]{:S(2)}) copy-start(f32[4,32,128]{2,1,0:T(8,128)} %reduce-scatter.2.cloned.1.call-done) | copy-start | bytes 196612
  439.8 9.4 %collective-permute-start.5 = (f32[5,32,128]{2,1,0:T(8,128)S(1)}, f32[5,32,128]{2,1,0:T(8,128)S(1)}, u32[]{:S(2)}, u32[]{:S(2)}) collective-permute-start(f32[5,32,128]{2,1,0:T(8,128)S(1)} %pad_maximum_fusion.4), channel_id=1, source_target_pairs={{0,32},{32,0},{64,96},{96,64},{128,160},{160,128},{192,224},{224,1... | collective-permute-start | bytes 245768 | tf_op jit(solution)/shard_map/ppermute | solution.py:14
  450.0 5.5 collective-permute-start.6
  455.6 5.7 %collective-permute-start.7 = (f32[3,32,128]{2,1,0:T(8,128)S(1)}, f32[3,32,128]{2,1,0:T(8,128)S(1)}, u32[]{:S(2)}, u32[]{:S(2)}) collective-permute-start(f32[3,32,128]{2,1,0:T(8,128)S(1)} %pad_maximum_fusion.6), channel_id=1, source_target_pairs={{0,128},{128,0},{32,160},{160,32},{64,192},{192,64},{96,224},{224,... | collective-permute-start | bytes 147464 | tf_op jit(solution)/shard_map/ppermute | solution.py:14
  461.3 9.0 %collective-permute-start.8 = (f32[2,32,128]{2,1,0:T(8,128)S(1)}, f32[2,32,128]{2,1,0:T(8,128)S(1)}, u32[]{:S(2)}, u32[]{:S(2)}) collective-permute-start(f32[2,32,128]{2,1,0:T(8,128)S(1)} %pad_maximum_fusion.7), channel_id=1, source_target_pairs={{0,256},{256,0},{32,288},{288,32},{64,320},{320,64},{96,352},{352,... | collective-permute-start | bytes 98312 | tf_op jit(solution)/shard_map/ppermute | solution.py:14
  476.4 40.4 %copy-start.8 = (f32[128,8,128]{0,2,1:T(8,128)S(1)}, f32[128,8,128]{0,2,1:T(8,128)}, u32[]{:S(2)}) copy-start(f32[128,8,128]{0,2,1:T(8,128)} %convolution_bitcast_fusion.1) | copy-start | bytes 1572868
  545.6 1.3 copy-start.4
  545.6 1.3 copy-start.5
  545.6 1.3 copy-start.6
  545.6 1.5 copy-start.7
Sparse Core Ops, SparseCore 0:
  152.6 286.2 reduce-scatter.1
  471.1 73.1 all-gather.2
where the time goes:
time: 561 us; the launch traced here: 556 us
  waiting for transfers between devices  409 us (73%)
  starting transfers between devices  55.3 us (10%)
  blocking collectives  36.5 us (7%)
  matrix products  18.2 us (3%)
  between operations  14.7 us (3%)
  other arithmetic  12.4 us (2%)
  local copies, waits for them, and re-layouts  9.91 us (2%)
    ppermute x9, waiting for transfers between devices, from_partner(): return lax.ppermute(block, axis, route)  282 us
    reduce_scatter x1, waiting for transfers between devices, per_device(): lax.psum_scatter(outer_flat, 'gy', scatter_dimension=1, tiled=True)  103 us
    ppermute x9, starting transfers between devices, from_partner(): return lax.ppermute(block, axis, route)  55.2 us
    all_gather x1, blocking collectives, per_device(): grad_rows = lax.all_gather(share_total, 'gy', axis=0, tiled=True)  36.5 us
    all_gather x1, waiting for transfers between devices, per_device(): lax.all_gather(part_stack.astype(jnp.bfloat16), 'gy', axis=1, tiled=True)  24.2 us
  transfers between devices with their start and end apart: 11, of which 10 were waited for; matrix products, arithmetic and copies ran while one was open for 4% of the time, Pallas kernels for 0%

commit v1 on v0

v1 whole, which is shorter than its diff:
```python
import jax
import jax.numpy as jnp
from jax import lax
from jax.experimental import pallas as pl
from jax.experimental.pallas import tpu as pltpu
from jax.sharding import PartitionSpec as P

MESH = pl.DeviceIdType.MESH
F32 = jnp.float32
BF16 = jnp.bfloat16
N = 128
HEADS = 8
KQ, KG, KT, KS, KU, KB, KV, KW, KC, KD = range(10)


def mm(a, b, ca, cb):
    return lax.dot_general(a, b, (((ca,), (cb,)), ((), ())), preferred_element_type=F32)


def nn(a, b):
    return mm(a, b, 1, 0)


def nt(a, b):
    return mm(a, b, 1, 1)


def tn(a, b):
    return mm(a, b, 0, 0)


def kernel(
    q_ref, k_ref, v_ref, g_ref, cls_ref, tab_ref,
    qo_ref, ko_ref, vo_ref,
    gates, lev_ref, st_send, qb, gb, sb, gtb, sq, qloc, kloc, vloc,
    lbuf, urecv, bsend, brecv, vsend, rbuf, ctr, dacc, csend, dsend, crecv, drecv,
    ssem, rsem,
):
    gx = lax.axis_index("gx")
    gy = lax.axis_index("gy")
    y = gx // 2
    core = gx % 2
    zz = gy // 8
    p = gy % 8
    a = core * 4 + zz

    def dev_p(r):
        return (gx, zz * 8 + r)

    def dev_a(r):
        return (y * 2 + r // 4, (r % 4) * 8 + p)

    def dev_y(r):
        return (r * 2 + core, gy)

    barrier = pltpu.get_barrier_semaphore()
    for i in range(1, 8):
        for dev in (dev_p((p + i) % 8), dev_a((a + i) % 8), dev_y((y + i) % 8)):
            pl.semaphore_signal(barrier, inc=1, device_id=dev, device_id_type=MESH)

    sends = []

    def send(kind, r, src, dst, slot, dev):
        copy = pltpu.make_async_remote_copy(
            src_ref=src, dst_ref=dst, send_sem=ssem.at[kind, r], recv_sem=rsem.at[kind, slot],
            device_id=dev, device_id_type=MESH,
        )
        copy.start()
        sends.append(copy)

    def local(kind, src, dst, slot):
        pltpu.make_async_copy(src, dst, rsem.at[kind, slot]).start()

    def arrived(kind, dst, slot):
        pltpu.make_async_copy(dst, dst, rsem.at[kind, slot]).wait()

    def cols(ref, r):
        return ref.at[:, pl.ds(pl.multiple_of(r * N, N), N)]

    classes = lax.broadcasted_iota(jnp.int32, (32, N), 0)
    onehot = (classes == cls_ref[...]).astype(F32)
    gates[...] = lax.dot_general(
        tab_ref[...], onehot, (((1,), (0,)), ((), ())),
        precision=lax.Precision.HIGHEST, preferred_element_type=F32,
    )
    brecv[y] = jnp.zeros((16, N), F32)

    pl.semaphore_wait(barrier, 21)

    for i in range(1, 8):
        r = (p + i) % 8
        send(KQ, i, cols(q_ref, r), qb.at[p], p, dev_p(r))
        send(KG, i, cols(g_ref, r), gb.at[p], p, dev_p(r))
        send(KT, i, gates.at[pl.ds(pl.multiple_of(r * 24 + 8, 8), 16), :], gtb.at[p], p, dev_p(r))
    local(KQ, cols(q_ref, p), qb.at[p], p)
    local(KG, cols(g_ref, p), gb.at[p], p)
    local(KT, gates.at[pl.ds(pl.multiple_of(p * 24 + 8, 8), 16), :], gtb.at[p], p)

    for h in range(HEADS):
        c = slice(h * N, h * N + N)
        st_send[h] = tn(k_ref[:, c], v_ref[:, c]).astype(BF16)
    for i in range(1, 8):
        r = (p + i) % 8
        send(KS, i, st_send.at[r], sb.at[p], p, dev_p(r))
    local(KS, st_send.at[p], sb.at[p], p)

    s_id = lax.broadcasted_iota(jnp.int32, (N, N), 0)
    t_id = lax.broadcasted_iota(jnp.int32, (N, N), 1)
    place = jnp.bitwise_xor(s_id, t_id)
    level = jnp.zeros((N, N), jnp.int32)
    for bit in range(7):
        level = level + (place >= 2**bit).astype(jnp.int32)
    lev_ref[...] = jnp.where(s_id <= t_id, level, -1)

    def own_head(h, _):
        c = pl.ds(pl.multiple_of(h * N, N), N)
        q = q_ref[:, c]
        k = k_ref[:, c]
        v = v_ref[:, c]
        g = g_ref[:, c]
        rows = gates[pl.ds(pl.multiple_of(h * 24, 8), 8), :]
        lev = lev_ref[...]
        w = jnp.zeros((N, N), F32)
        for l in range(8):
            w = jnp.where(lev == l, rows[l : l + 1, :], w)
        wg = (w * nt(v, g)).astype(BF16)
        ws = (w * nt(k, q)).astype(BF16)
        kloc[:, c] = nn(wg, q)
        vloc[:, c] = nn(ws, g)
        qloc[:, c] = tn(wg, k)
        return 0

    lax.fori_loop(0, HEADS, own_head, 0)

    low = {}
    for r in range(8):
        arrived(KQ, qb.at[r], r)
        arrived(KG, gb.at[r], r)
        arrived(KT, gtb.at[r], r)
        qt = qb[r].T.astype(F32)
        rows = gtb[r]
        for l in range(3, 9):
            sq[(l - 3) * N : (l - 2) * N, r * N : (r + 1) * N] = (qt * rows[l : l + 1, :]).astype(BF16)
        for l in range(3):
            if r >> l & 1:
                part = nn((qt * rows[l : l + 1, :]).astype(BF16), gb[r])
                key = (l, r >> l)
                low[key] = low[key] + part if key in low else part
    for b in range(8):
        acc = jnp.zeros((N, N), F32)
        for l in range(3):
            if not b >> l & 1:
                acc = acc + low[(l, (b >> l) ^ 1)]
        dacc[b] = acc
    grads = nn(sq[...], gb[...].reshape(8 * N, N))
    lbuf[1:7] = grads.astype(BF16).reshape(6, N, N)
    states = []
    for r in range(8):
        arrived(KS, sb.at[r], r)
        states.append(sb[r].astype(F32))
    pair = [states[2 * j] + states[2 * j + 1] for j in range(4)]
    quad = [pair[0] + pair[1], pair[2] + pair[3]]
    lbuf[0] = (quad[0] + quad[1]).astype(BF16)
    for i in range(1, 8):
        r = (a + i) % 8
        send(KU, i, lbuf.at[:, pl.ds(pl.multiple_of(r * 16, 16), 16), :], urecv.at[a], a, dev_a(r))
    local(KU, lbuf.at[:, pl.ds(pl.multiple_of(a * 16, 16), 16), :], urecv.at[a], a)

    for b in range(8):
        acc = jnp.zeros((N, N), F32)
        rows = gtb[b]
        for l in range(3):
            if b >> l & 1:
                other = (b >> l) ^ 1
                left = sb[other] if l == 0 else (pair, quad)[l - 1][other].astype(BF16)
                acc = acc + rows[l : l + 1, :] * nt(left, gb[b])
        ctr[b] = acc

    tops = []
    lows = {l: [] for l in range(3, 9)}
    for r in range(8):
        arrived(KU, urecv.at[r], r)
        tops.append(urecv[r, 0].astype(F32))
        for l in range(3, 9):
            lows[l].append(urecv[r, l - 2].astype(F32))
    tpair = [tops[2 * j] + tops[2 * j + 1] for j in range(4)]
    tquad = [tpair[0] + tpair[1], tpair[2] + tpair[3]]
    bsend[0] = tquad[0] + tquad[1]
    for l in range(6, 9):
        total = lows[l][0]
        for r in range(1, 8):
            total = total + lows[l][r]
        bsend[l - 5] = total
    for i in range(1, 8):
        r = (y + i) % 8
        high = jnp.where(y // 4 != r // 4, 3, jnp.where(y // 2 != r // 2, 2, 1))
        pick = jnp.where(y < r, 0, high)
        send(KB, i, bsend.at[pick], brecv.at[y], y, dev_y(r))
    zero = jnp.zeros((16, N), F32)
    l4 = {3: lows[4][2] + lows[4][3], 7: lows[4][6] + lows[4][7]}
    l5 = (lows[5][4] + lows[5][5]) + (lows[5][6] + lows[5][7])
    dmid = []
    for r in range(8):
        vsend[r, 0] = (tops[r - 1] if r & 1 else zero).astype(BF16)
        vsend[r, 1] = (tpair[(r >> 1) ^ 1] if r & 2 else zero).astype(BF16)
        vsend[r, 2] = (tquad[0] if r & 4 else zero).astype(BF16)
        acc = zero
        if not r & 1:
            acc = acc + lows[3][r + 1]
        if not r & 2:
            acc = acc + l4[r | 3]
        if not r & 4:
            acc = acc + l5
        dmid.append(acc)
    mine = pl.ds(pl.multiple_of(a * 16, 16), 16)
    for i in range(1, 8):
        r = (a + i) % 8
        send(KV, i, vsend.at[r, pl.ds(0, 3)], rbuf.at[pl.ds(0, 3), mine, :], a, dev_a(r))
    local(KV, vsend.at[a, pl.ds(0, 3)], rbuf.at[pl.ds(0, 3), mine, :], a)

    for r in range(8):
        arrived(KV, rbuf.at[pl.ds(0, 3), pl.ds(16 * r, 16), :], r)

    def middle(b, _):
        rows = gtb[b]
        prod = nt(rbuf[0:3].reshape(3 * N, N), gb[b])
        acc = ctr[b]
        for l in range(3):
            acc = acc + rows[3 + l : 4 + l, :] * prod[l * N : (l + 1) * N]
        ctr[b] = acc
        return 0

    lax.fori_loop(0, 8, middle, 0, unroll=2)

    for i in range(1, 8):
        arrived(KB, brecv.at[(y + i) % 8], (y + i) % 8)
    s6, s7, s8, dtop = zero, zero, zero, zero
    for r in range(8):
        got = brecv[r]
        before = r < y
        s6 = s6 + jnp.where(jnp.logical_and(before, r // 2 == y // 2), got, 0.0)
        s7 = s7 + jnp.where(
            jnp.logical_and(before, jnp.logical_and(r // 4 == y // 4, r // 2 != y // 2)), got, 0.0
        )
        s8 = s8 + jnp.where(jnp.logical_and(before, r // 4 != y // 4), got, 0.0)
        dtop = dtop + jnp.where(r > y, got, 0.0)
    for r in range(8):
        vsend[r, 3] = s6.astype(BF16)
        vsend[r, 4] = s7.astype(BF16)
        vsend[r, 5] = s8.astype(BF16)
        vsend[r, 6] = (dmid[r] + dtop).astype(BF16)
    for i in range(1, 8):
        r = (a + i) % 8
        send(KW, i, vsend.at[r, pl.ds(3, 4)], rbuf.at[pl.ds(3, 4), mine, :], a, dev_a(r))
    local(KW, vsend.at[a, pl.ds(3, 4)], rbuf.at[pl.ds(3, 4), mine, :], a)
    for r in range(8):
        arrived(KW, rbuf.at[pl.ds(3, 4), pl.ds(16 * r, 16), :], r)

    for b in range(8):
        dsend[b] = (dacc[b] + rbuf[6].astype(F32)).astype(BF16)
    for i in range(1, 8):
        r = (p + i) % 8
        send(KD, i, dsend.at[r], drecv.at[p], p, dev_p(r))
    local(KD, dsend.at[p], drecv.at[p], p)

    def upper(b, _):
        rows = gtb[b]
        prod = nt(rbuf[3:6].reshape(3 * N, N), gb[b])
        acc = ctr[b]
        for l in range(3):
            acc = acc + rows[6 + l : 7 + l, :] * prod[l * N : (l + 1) * N]
        csend[b] = acc.T.astype(BF16)
        return 0

    lax.fori_loop(0, 8, upper, 0, unroll=2)
    for i in range(1, 8):
        r = (p + i) % 8
        send(KC, i, csend.at[r], crecv.at[p], p, dev_p(r))
    local(KC, csend.at[p], crecv.at[p], p)

    for h in range(HEADS):
        c = slice(h * N, h * N + N)
        arrived(KD, drecv.at[h], h)
        d = drecv[h]
        ko_ref[:, c] = (kloc[:, c] + nt(v_ref[:, c], d)).astype(BF16)
        vo_ref[:, c] = (vloc[:, c] + nn(k_ref[:, c], d)).astype(BF16)
    for h in range(HEADS):
        c = slice(h * N, h * N + N)
        arrived(KC, crecv.at[h], h)
        qo_ref[:, c] = (qloc[:, c] + crecv[h].astype(F32)).astype(BF16)
    for copy in sends:
        copy.wait_send()


def per_device(query_rows, key_rows, value_rows, out_grad, gate_class, gate_table):
    table = jnp.pad(gate_table.transpose(2, 1, 0), ((0, 0), (0, 4), (0, 0))).reshape(24 * HEADS, 32)
    out = jax.ShapeDtypeStruct((N, HEADS * N), BF16)
    vmem = pl.BlockSpec(memory_space=pltpu.VMEM)
    cube = lambda n, dtype: pltpu.VMEM((n, N, N), dtype)
    wide = pltpu.VMEM((N, HEADS * N), F32)
    return pl.pallas_call(
        kernel,
        out_shape=(out, out, out),
        in_specs=[vmem] * 6,
        out_specs=(vmem, vmem, vmem),
        scratch_shapes=[
            pltpu.VMEM((24 * HEADS, N), F32),
            pltpu.VMEM((N, N), jnp.int32),
            cube(8, BF16), cube(8, BF16), cube(8, BF16), cube(8, BF16),
            pltpu.VMEM((8, 16, N), F32),
            pltpu.VMEM((6 * N, 8 * N), BF16),
            wide, wide, wide,
            cube(7, BF16),
            pltpu.VMEM((8, 7, 16, N), BF16),
            pltpu.VMEM((4, 16, N), F32),
            pltpu.VMEM((8, 16, N), F32),
            pltpu.VMEM((8, 7, 16, N), BF16),
            cube(7, BF16),
            cube(8, F32), cube(8, F32),
            cube(8, BF16), cube(8, BF16), cube(8, BF16), cube(8, BF16),
            pltpu.SemaphoreType.DMA((10, 8)),
            pltpu.SemaphoreType.DMA((10, 8)),
        ],
        compiler_params=pltpu.CompilerParams(
            collective_id=0, has_side_effects=True, vmem_limit_bytes=40 * 1024 * 1024
        ),
    )(query_rows, key_rows, value_rows, out_grad, gate_class.reshape(1, N), table)


def solution(mesh):
    rows = P(("gx", "gy"), None)
    return jax.shard_map(
        per_device,
        mesh=mesh,
        in_specs=(rows, rows, rows, rows, P(("gx", "gy")), P()),
        out_specs=(rows, rows, rows),
        check_vma=False,
    )
```

time: 561 us -> 61.7 us (0.11)
  waiting for transfers between devices: 409 us -> 0 us
  starting transfers between devices: 55.3 us -> 0 us
  Pallas kernels: 0 us -> 54.2 us
  blocking collectives: 36.5 us -> 0 us
  matrix products: 18.2 us -> 0 us
  between operations: 14.7 us -> 0.68 us
  other arithmetic: 12.4 us -> 0 us
    ppermute x9 -> x0, waiting for transfers between devices: 282 us -> none  [from_partner(): return lax.ppermute(block, axis, route)]
    reduce_scatter x1 -> x0, waiting for transfers between devices: 103 us -> none  [per_device(): lax.psum_scatter(outer_flat, 'gy', scatter_dimension=1, tiled=True)]
    ppermute x9 -> x0, starting transfers between devices: 55.2 us -> none  [from_partner(): return lax.ppermute(block, axis, route)]
    pallas_call x0 -> x1, Pallas kernels: none -> 54.2 us  [per_device(): pl.pallas_call(kernel, out_shape=(out, out, out), in_specs=[vmem] * 6, ou...]
    all_gather x1 -> x0, blocking collectives: 36.5 us -> none  [per_device(): grad_rows = lax.all_gather(share_total, 'gy', axis=0, tiled=True)]
    all_gather x1 -> x0, waiting for transfers between devices: 24.2 us -> none  [per_device(): lax.all_gather(part_stack.astype(jnp.bfloat16), 'gy', axis=1, tiled=True)]
    dot_general x18 -> x0, matrix products: 18.2 us -> none  [the longest x9 10.2 us: per_device(): jnp.einsum('the,hde->thd', grad_heads, rounded_states[tree_level], prefer...]
  transfers between devices with their start and end apart: 11 -> 0, of which waited for: 10 -> 0; matrix products, arithmetic and copies ran while one was open for 4% -> 0% of each run, Pallas kernels for 0% -> 0%
where the time goes in v1:
time: 61.7 us; the launch traced here: 61.4 us
  Pallas kernels  54.2 us (88%)
  local copies, waits for them, and re-layouts  6.56 us (11%)
  between operations  0.68 us (1%)
    pallas_call x1, Pallas kernels, per_device(): pl.pallas_call(kernel, out_shape=(out, out, out), in_specs=[vmem] * 6, ou...  54.2 us
    unnamed x14, local copies, waits for them, and re-layouts  6.55 us

profile of v1, /device:TPU:1, one launch (start us, length us, event | category | flops | bytes accessed | tf_op | source)
XLA Modules:
  0.0 61.4 jit_solution(3310187283997810022)
XLA Ops:
  0.6 0.0 copy-start
  0.6 0.9 %copy.10 = f32[8,20,32]{2,1,0:T(8,128)S(1)} copy(f32[8,20,32]{2,0,1:T(8,128)} %bitcast.5) | data formatting | bytes 40960
  1.6 0.0 copy-start.4
  1.6 0.0 copy-done
  1.6 0.6 %copy-done.4 = s32[128]{0:T(128)S(1)} copy-done((s32[128]{0:T(128)S(1)}, s32[128]{0:T(128)}, u32[]{:S(2)}) %copy-start.4) | copy-done | bytes 536
  2.3 0.0 copy-start.1
  2.3 0.9 %copy-done.1 = bf16[128,1024]{1,0:T(8,128)(2,1)S(1)} copy-done((bf16[128,1024]{1,0:T(8,128)(2,1)S(1)}, bf16[128,1024]{1,0:T(8,128)(2,1)}, u32[]{:S(2)}) %copy-start.1) | copy-done | bytes 262168
  3.2 0.0 copy-start.2
  3.2 0.9 %copy-done.2 = bf16[128,1024]{1,0:T(8,128)(2,1)S(1)} copy-done((bf16[128,1024]{1,0:T(8,128)(2,1)S(1)}, bf16[128,1024]{1,0:T(8,128)(2,1)}, u32[]{:S(2)}) %copy-start.2) | copy-done | bytes 262168
  4.2 0.0 copy-start.3
  4.2 0.9 %copy-done.3 = bf16[128,1024]{1,0:T(8,128)(2,1)S(1)} copy-done((bf16[128,1024]{1,0:T(8,128)(2,1)S(1)}, bf16[128,1024]{1,0:T(8,128)(2,1)}, u32[]{:S(2)}) %copy-start.3) | copy-done | bytes 262168
  5.1 54.2 %shard_map.85 = (bf16[128,1024]{1,0:T(8,128)(2,1)S(1)}, bf16[128,1024]{1,0:T(8,128)(2,1)S(1)}, bf16[128,1024]{1,0:T(8,128)(2,1)S(1)}) custom-call(bf16[128,1024]{1,0:T(8,128)(2,1)S(1)} %copy-done, bf16[128,1024]{1,0:T(8,128)(2,1)S(1)} %copy-done.1, bf16[128,1024]{1,0:T(8,128)(2,1)S(1)} %copy-done.2, bf16[128,1024]{1,0:T(8,128)(2,1)S(1)} %copy-done.3, ...), custom_call_target="tpu_custom_call" | custom-call | tf_op jit(solution)/shard_map/pallas_call | solution.py:301
  59.3 0.7 %copy.14 = bf16[128,1024]{1,0:T(8,128)(2,1)} copy(bf16[128,1024]{1,0:T(8,128)(2,1)S(1)} %get-tuple-element.6) | data formatting | bytes 524288
  60.0 0.7 %copy.15 = bf16[128,1024]{1,0:T(8,128)(2,1)} copy(bf16[128,1024]{1,0:T(8,128)(2,1)S(1)} %get-tuple-element.7) | data formatting | bytes 524288
  60.7 0.7 %copy.16 = bf16[128,1024]{1,0:T(8,128)(2,1)} copy(bf16[128,1024]{1,0:T(8,128)(2,1)S(1)} %get-tuple-element.8) | data formatting | bytes 524288
  (1 shorter events, 0.0 us)
Async XLA Ops:
  0.6 1.0 %copy-start = (bf16[128,1024]{1,0:T(8,128)(2,1)S(1)}, bf16[128,1024]{1,0:T(8,128)(2,1)}, u32[]{:S(2)}) copy-start(bf16[128,1024]{1,0:T(8,128)(2,1)} %q_ref.1) | copy-start | bytes 786436
  1.6 0.7 %copy-start.4 = (s32[128]{0:T(128)S(1)}, s32[128]{0:T(128)}, u32[]{:S(2)}) copy-start(s32[128]{0:T(128)} %param.10) | copy-start | bytes 1540
  2.3 0.9 %copy-start.1 = (bf16[128,1024]{1,0:T(8,128)(2,1)S(1)}, bf16[128,1024]{1,0:T(8,128)(2,1)}, u32[]{:S(2)}) copy-start(bf16[128,1024]{1,0:T(8,128)(2,1)} %k_ref.1) | copy-start | bytes 786436
  3.2 0.9 %copy-start.2 = (bf16[128,1024]{1,0:T(8,128)(2,1)S(1)}, bf16[128,1024]{1,0:T(8,128)(2,1)}, u32[]{:S(2)}) copy-start(bf16[128,1024]{1,0:T(8,128)(2,1)} %v_ref.1) | copy-start | bytes 786436
  4.2 0.9 %copy-start.3 = (bf16[128,1024]{1,0:T(8,128)(2,1)S(1)}, bf16[128,1024]{1,0:T(8,128)(2,1)}, u32[]{:S(2)}) copy-start(bf16[128,1024]{1,0:T(8,128)(2,1)} %g_ref.1) | copy-start | bytes 786436

commit v2 on v1

v2 whole, which is shorter than its diff:
```python
import jax
import jax.numpy as jnp
from jax import lax
from jax.experimental import pallas as pl
from jax.experimental.pallas import tpu as pltpu
from jax.sharding import PartitionSpec as P

MESH = pl.DeviceIdType.MESH
F32 = jnp.float32
BF16 = jnp.bfloat16
N = 128
HEADS = 8
KQ, KG, KT, KS, KL, KU, KB, KV, KW, KX, KC, KD = 0, 1, 2, 3, 4, 10, 11, 12, 15, 16, 19, 20
KINDS = 21
NEAR = ((0, 1), (0, 3), (1, 0), (1, 1), (1, 3), (0, 2), (1, 2))
FAR = ((0, 2), (1, 2), (0, 1), (0, 3), (1, 1), (1, 3), (1, 0))


def mm(a, b, ca, cb):
    return lax.dot_general(a, b, (((ca,), (cb,)), ((), ())), preferred_element_type=F32)


def nn(a, b):
    return mm(a, b, 1, 0)


def nt(a, b):
    return mm(a, b, 1, 1)


def tn(a, b):
    return mm(a, b, 0, 0)


def kernel(
    q_hbm, k_hbm, v_hbm, g_hbm, cls_hbm, tab_hbm,
    qo_ref, ko_ref, vo_ref,
    q_ref, k_ref, v_ref, g_ref, cls_ref, tab_ref,
    gates, hg, lev_ref, st_send, qb, gb, sb, gtb, lacc, qloc, kloc, vloc,
    lbuf, urecv, bsend, brecv, ysum, vsend, wsend, xsend, rbuf, ctr, dacc, csend, dsend, crecv, drecv,
    lsem, ssem, rsem,
):
    gx = lax.axis_index("gx")
    gy = lax.axis_index("gy")
    y = gx // 2
    core = gx % 2
    zz = gy // 8
    p = gy % 8
    z0 = p // 4
    x = p % 4
    a = core * 4 + zz
    flag = {3: zz % 2, 4: zz // 2, 5: core, 6: y % 2, 7: y // 2 % 2, 8: y // 4}
    near = [(z0 + dz) % 2 * 4 + (x + dx) % 4 for dz, dx in NEAR]
    far = [(core + dc) % 2 * 4 + (zz + dz) % 4 for dc, dz in FAR]

    def dev_p(r):
        return (gx, zz * 8 + r)

    def dev_a(r):
        return (y * 2 + r // 4, (r % 4) * 8 + p)

    def dev_y(r):
        return (r * 2 + core, gy)

    barrier = pltpu.get_barrier_semaphore()
    for i in range(7):
        for dev in (dev_p(near[i]), dev_a(far[i]), dev_y((y + i + 1) % 8)):
            pl.semaphore_signal(barrier, inc=1, device_id=dev, device_id_type=MESH)

    loads = []
    for i, (src, dst) in enumerate((
        (cls_hbm, cls_ref), (tab_hbm, tab_ref), (q_hbm, q_ref), (g_hbm, g_ref), (k_hbm, k_ref), (v_hbm, v_ref),
    )):
        loads.append(pltpu.make_async_copy(src, dst, lsem.at[i]))
        loads[-1].start()

    sends = []

    def send(kind, i, src, dst, slot, dev, keep=sends):
        pltpu.make_async_remote_copy(
            src_ref=src, dst_ref=dst, send_sem=ssem.at[kind, i], recv_sem=rsem.at[kind, slot],
            device_id=dev, device_id_type=MESH,
        ).start()
        keep.append((kind, i))

    def sent(done):
        for kind, i in done:
            if kind < KL and kind != KT or kind >= KC:
                like = qb.at[0]
            elif kind == KT:
                like = gtb.at[0]
            elif kind == KB:
                like = brecv.at[0]
            else:
                like = urecv.at[0, 0]
            pltpu.make_async_copy(like, like, ssem.at[kind, i]).wait()

    def local(kind, src, dst, slot):
        pltpu.make_async_copy(src, dst, rsem.at[kind, slot]).start()

    def arrived(kind, dst, slot):
        pltpu.make_async_copy(dst, dst, rsem.at[kind, slot]).wait()

    def cols(ref, r):
        return ref.at[:, pl.ds(pl.multiple_of(r * N, N), N)]

    def rows16(r):
        return pl.ds(pl.multiple_of(r * 16, 16), 16)

    zero = jnp.zeros((16, N), F32)
    for l in range(3, 9):
        @pl.when(flag[l] == 0)
        def _():
            rbuf[l - 3] = jnp.zeros((N, N), BF16)
    loads[0].wait()
    loads[1].wait()
    classes = lax.broadcasted_iota(jnp.int32, (32, N), 0)
    onehot = (classes == cls_ref[...]).astype(F32)
    gates[...] = lax.dot_general(
        tab_ref[...].reshape(20 * HEADS, 32), onehot, (((1,), (0,)), ((), ())),
        precision=lax.Precision.HIGHEST, preferred_element_type=F32,
    )
    for h in range(HEADS):
        hg[h, 0:20] = gates[pl.ds(h, 20, stride=HEADS), :]
        hg[h, 20:24] = jnp.zeros((4, N), F32)
    loads[2].wait()
    loads[3].wait()

    pl.semaphore_wait(barrier, 21)

    for i, r in enumerate(near):
        send(KQ, i, cols(q_ref, r), qb.at[p], p, dev_p(r))
        send(KG, i, cols(g_ref, r), gb.at[p], p, dev_p(r))
        send(KT, i, hg.at[r, pl.ds(8, 16)], gtb.at[p], p, dev_p(r))
    local(KQ, cols(q_ref, p), qb.at[p], p)
    local(KG, cols(g_ref, p), gb.at[p], p)
    local(KT, hg.at[p, pl.ds(8, 16)], gtb.at[p], p)

    loads[4].wait()
    loads[5].wait()
    for h in range(HEADS):
        c = slice(h * N, h * N + N)
        st_send[h] = tn(k_ref[:, c], v_ref[:, c]).astype(BF16)
    for i, r in enumerate(near):
        send(KS, i, st_send.at[r], sb.at[p], p, dev_p(r))
    local(KS, st_send.at[p], sb.at[p], p)

    s_id = lax.broadcasted_iota(jnp.int32, (N, N), 0)
    t_id = lax.broadcasted_iota(jnp.int32, (N, N), 1)
    place = jnp.bitwise_xor(s_id, t_id)
    level = jnp.zeros((N, N), jnp.int32)
    for bit in range(7):
        level = level + (place >= 2**bit).astype(jnp.int32)
    lev_ref[...] = jnp.where(s_id <= t_id, level, -1)

    def own_head(h, _):
        c = pl.ds(pl.multiple_of(h * N, N), N)
        q = q_ref[:, c]
        k = k_ref[:, c]
        v = v_ref[:, c]
        g = g_ref[:, c]
        rows = hg[h, 0:8]
        lev = lev_ref[...]
        w = jnp.zeros((N, N), F32)
        for l in range(8):
            w = jnp.where(lev == l, rows[l : l + 1, :], w)
        wg = (w * nt(v, g)).astype(BF16)
        ws = (w * nt(k, q)).astype(BF16)
        kloc[:, c] = nn(wg, q)
        vloc[:, c] = nn(ws, g)
        qloc[:, c] = tn(wg, k)
        return 0

    lax.fori_loop(0, 4, own_head, 0)

    for i, r in enumerate([p] + near):
        arrived(KQ, qb.at[r], r)
        arrived(KG, gb.at[r], r)
        arrived(KT, gtb.at[r], r)
        qt = qb[r].T.astype(F32)
        rows = gtb[r]
        scaled = jnp.concatenate([(qt * rows[l : l + 1, :]).astype(BF16) for l in range(3, 9)], axis=0)
        part = nn(scaled, gb[r])
        if i == 0:
            lacc[...] = part
        elif i < 7:
            lacc[...] += part
        else:
            lbuf[1:7] = (lacc[...] + part).astype(BF16).reshape(6, N, N)
    kept = {}
    for l in range(8, 2, -1):
        kept[l] = []
        @pl.when(flag[l] == 1)
        def _():
            for i, r in enumerate(far):
                send(KL + l - 3, i, lbuf.at[l - 2, rows16(r), :], urecv.at[a, l - 2], a, dev_a(r), kept[l])
            local(KL + l - 3, lbuf.at[l - 2, rows16(a), :], urecv.at[a, l - 2], a)

    states = []
    for r in range(8):
        arrived(KS, sb.at[r], r)
        states.append(sb[r].astype(F32))
    pair = [states[2 * j] + states[2 * j + 1] for j in range(4)]
    quad = [pair[0] + pair[1], pair[2] + pair[3]]
    lbuf[0] = (quad[0] + quad[1]).astype(BF16)
    for i, r in enumerate(far):
        send(KU, i, lbuf.at[0, rows16(r), :], urecv.at[a, 0], a, dev_a(r))
    local(KU, lbuf.at[0, rows16(a), :], urecv.at[a, 0], a)

    lax.fori_loop(4, HEADS, own_head, 0)

    lows = {}
    for l in range(3, 6):
        for r in range(8):
            if r >> (l - 3) & 1:
                arrived(KL + l - 3, urecv.at[r, l - 2], r)
                lows[l, r] = urecv[r, l - 2].astype(F32)
    for l in range(6, 9):
        @pl.when(flag[l] == 1)
        def _():
            total = zero
            for r in range(8):
                arrived(KL + l - 3, urecv.at[r, l - 2], r)
                total = total + urecv[r, l - 2].astype(F32)
            bsend[l - 5] = total
    down = []
    for r in range(8):
        down.append([])
        @pl.when(r < y)
        def _():
            high = jnp.where(y // 4 != r // 4, 3, jnp.where(y // 2 != r // 2, 2, 1))
            send(KB, r, bsend.at[high], brecv.at[y], y, dev_y(r), down[r])
    l4 = {3: lows[4, 2] + lows[4, 3], 7: lows[4, 6] + lows[4, 7]}
    l5 = (lows[5, 4] + lows[5, 5]) + (lows[5, 6] + lows[5, 7])
    dmid = []
    for r in range(8):
        acc = zero
        if not r & 1:
            acc = acc + lows[3, r + 1]
        if not r & 2:
            acc = acc + l4[r | 3]
        if not r & 4:
            acc = acc + l5
        dmid.append(acc)

    tops = []
    for r in range(8):
        arrived(KU, urecv.at[r, 0], r)
        tops.append(urecv[r, 0].astype(F32))
    tpair = [tops[2 * j] + tops[2 * j + 1] for j in range(4)]
    tquad = [tpair[0] + tpair[1], tpair[2] + tpair[3]]
    bsend[0] = tquad[0] + tquad[1]
    up = []
    for r in range(8):
        up.append([])
        @pl.when(r > y)
        def _():
            send(KB, r, bsend.at[0], brecv.at[y], y, dev_y(r), up[r])
    for r in range(8):
        if r & 1:
            vsend[r, 0] = tops[r - 1].astype(BF16)
        if r & 2:
            vsend[r, 1] = tpair[(r >> 1) ^ 1].astype(BF16)
        if r & 4:
            vsend[r, 2] = tquad[0].astype(BF16)
    side = {}
    for i, r in enumerate(far):
        for l in range(3):
            side[i, l] = []
            @pl.when(r // 2**l % 2 == 1)
            def _():
                send(KV + l, i, vsend.at[r, l], rbuf.at[l, rows16(a), :], a, dev_a(r), side[i, l])
    for l in range(3):
        @pl.when(flag[3 + l] == 1)
        def _():
            local(KV + l, vsend.at[a, l], rbuf.at[l, rows16(a), :], a)

    low = {}
    for r in range(1, 8):
        qt = qb[r].T.astype(F32)
        rows = gtb[r]
        for l in range(3):
            if r >> l & 1:
                part = nn((qt * rows[l : l + 1, :]).astype(BF16), gb[r])
                key = (l, r >> l)
                low[key] = low[key] + part if key in low else part
    for b in range(8):
        acc = jnp.zeros((N, N), F32)
        for l in range(3):
            if not b >> l & 1:
                acc = acc + low[(l, (b >> l) ^ 1)]
        dacc[b] = acc
    pair = [sb[2 * j].astype(F32) + sb[2 * j + 1].astype(F32) for j in range(4)]
    for b in range(8):
        acc = jnp.zeros((N, N), F32)
        rows = gtb[b]
        for l in range(3):
            if b >> l & 1:
                other = (b >> l) ^ 1
                if l == 0:
                    left = sb[other]
                elif l == 1:
                    left = pair[other].astype(BF16)
                else:
                    left = (pair[0] + pair[1]).astype(BF16)
                acc = acc + rows[l : l + 1, :] * nt(left, gb[b])
        ctr[b] = acc

    ysum[...] = jnp.zeros((4, 16, N), F32)
    for r in range(1, 8):
        @pl.when(r > y)
        def _():
            arrived(KB, brecv.at[r], r)
            ysum[3] += brecv[r]
    dtop = ysum[3]
    for r in range(8):
        wsend[r] = (dmid[r] + dtop).astype(BF16)
    for i, r in enumerate(far):
        send(KW, i, wsend.at[r], rbuf.at[6, rows16(a), :], a, dev_a(r))
    local(KW, wsend.at[a], rbuf.at[6, rows16(a), :], a)

    for r in range(7):
        @pl.when(r < y)
        def _():
            arrived(KB, brecv.at[r], r)
            high = jnp.where(y // 4 != r // 4, 2, jnp.where(y // 2 != r // 2, 1, 0))
            ysum[high] += brecv[r]
    for l in range(3):
        xsend[l] = ysum[l].astype(BF16)
    for l in range(3):
        kept[9 + l] = []
        @pl.when(flag[6 + l] == 1)
        def _():
            for i, r in enumerate(far):
                send(KX + l, i, xsend.at[l], rbuf.at[3 + l, rows16(a), :], a, dev_a(r), kept[9 + l])
            local(KX + l, xsend.at[l], rbuf.at[3 + l, rows16(a), :], a)

    for l in range(3):
        @pl.when(flag[3 + l] == 1)
        def _():
            for r in range(8):
                arrived(KV + l, rbuf.at[l, pl.ds(16 * r, 16), :], r)

    def middle(b, _):
        rows = gtb[b]
        prod = nt(rbuf[0:3].reshape(3 * N, N), gb[b])
        acc = ctr[b]
        for l in range(3):
            acc = acc + rows[3 + l : 4 + l, :] * prod[l * N : (l + 1) * N]
        ctr[b] = acc
        return 0

    lax.fori_loop(0, 8, middle, 0, unroll=2)

    for r in range(8):
        arrived(KW, rbuf.at[6, pl.ds(16 * r, 16), :], r)
    for b in range(8):
        dsend[b] = (dacc[b] + rbuf[6].astype(F32)).astype(BF16)
    for i, r in enumerate(near):
        send(KD, i, dsend.at[r], drecv.at[p], p, dev_p(r))
    local(KD, dsend.at[p], drecv.at[p], p)

    for l in range(3):
        @pl.when(flag[6 + l] == 1)
        def _():
            for r in range(8):
                arrived(KX + l, rbuf.at[3 + l, pl.ds(16 * r, 16), :], r)

    for i, b in enumerate(near + [p]):
        rows = gtb[b]
        prod = nt(rbuf[3:6].reshape(3 * N, N), gb[b])
        acc = ctr[b]
        for l in range(3):
            acc = acc + rows[6 + l : 7 + l, :] * prod[l * N : (l + 1) * N]
        csend[b] = acc.T.astype(BF16)
        if i < 7:
            send(KC, i, csend.at[b], crecv.at[p], p, dev_p(b))
    local(KC, csend.at[p], crecv.at[p], p)

    for h in range(HEADS):
        c = slice(h * N, h * N + N)
        arrived(KD, drecv.at[h], h)
        d = drecv[h]
        ko_ref[:, c] = (kloc[:, c] + nt(v_ref[:, c], d)).astype(BF16)
        vo_ref[:, c] = (vloc[:, c] + nn(k_ref[:, c], d)).astype(BF16)
    for h in range(HEADS):
        c = slice(h * N, h * N + N)
        arrived(KC, crecv.at[h], h)
        qo_ref[:, c] = (qloc[:, c] + crecv[h].astype(F32)).astype(BF16)

    sent(sends)
    for l in range(3, 12):
        @pl.when(flag[l if l < 9 else l - 3] == 1)
        def _():
            sent(kept[l])
    for r in range(8):
        @pl.when(r < y)
        def _():
            sent(down[r])
        @pl.when(r > y)
        def _():
            sent(up[r])
    for i, r in enumerate(far):
        for l in range(3):
            @pl.when(r // 2**l % 2 == 1)
            def _():
                sent(side[i, l])


def write_out(qi, ki, vi, qo, ko, vo, sem):
    copies = [pltpu.make_async_copy(s, d, sem.at[i]) for i, (s, d) in enumerate(((qi, qo), (ki, ko), (vi, vo)))]
    for copy in copies:
        copy.start()
    for copy in copies:
        copy.wait()


def per_device(query_rows, key_rows, value_rows, out_grad, gate_class, gate_table):
    table = gate_table.transpose(1, 2, 0)
    out = jax.ShapeDtypeStruct((N, HEADS * N), BF16)
    vmem = pl.BlockSpec(memory_space=pltpu.VMEM)
    hbm = pl.BlockSpec(memory_space=pltpu.HBM)
    cube = lambda n, dtype: pltpu.VMEM((n, N, N), dtype)
    wide = pltpu.VMEM((N, HEADS * N), F32)
    flat = pltpu.VMEM((N, HEADS * N), BF16)
    outs = pl.pallas_call(
        kernel,
        out_shape=(out, out, out),
        in_specs=[hbm] * 6,
        out_specs=(vmem, vmem, vmem),
        scratch_shapes=[
            flat, flat, flat, flat,
            pltpu.VMEM((1, N), jnp.int32),
            pltpu.VMEM((20, HEADS, 32), F32),
            pltpu.VMEM((20 * HEADS, N), F32),
            pltpu.VMEM((HEADS, 24, N), F32),
            pltpu.VMEM((N, N), jnp.int32),
            cube(8, BF16), cube(8, BF16), cube(8, BF16), cube(8, BF16),
            pltpu.VMEM((8, 16, N), F32),
            pltpu.VMEM((6 * N, N), F32),
            wide, wide, wide,
            cube(7, BF16),
            pltpu.VMEM((8, 7, 16, N), BF16),
            pltpu.VMEM((4, 16, N), F32),
            pltpu.VMEM((8, 16, N), F32),
            pltpu.VMEM((4, 16, N), F32),
            pltpu.VMEM((8, 3, 16, N), BF16),
            pltpu.VMEM((8, 16, N), BF16),
            pltpu.VMEM((3, 16, N), BF16),
            cube(7, BF16),
            cube(8, F32), cube(8, F32),
            cube(8, BF16), cube(8, BF16), cube(8, BF16), cube(8, BF16),
            pltpu.SemaphoreType.DMA((6,)),
            pltpu.SemaphoreType.DMA((KINDS, 8)),
            pltpu.SemaphoreType.DMA((KINDS, 8)),
        ],
        compiler_params=pltpu.CompilerParams(
            collective_id=0, has_side_effects=True, vmem_limit_bytes=40 * 1024 * 1024
        ),
    )(*[pltpu.with_memory_space_constraint(one, pltpu.HBM) for one in (query_rows, key_rows, value_rows, out_grad, gate_class.reshape(1, N), table)])
    return pl.pallas_call(
        write_out,
        out_shape=(out, out, out),
        in_specs=[vmem] * 3,
        out_specs=(hbm, hbm, hbm),
        compiler_params=pltpu.CompilerParams(vmem_limit_bytes=16 * 1024 * 1024),
        scratch_shapes=[pltpu.SemaphoreType.DMA((3,))],
    )(*outs)


def solution(mesh):
    rows = P(("gx", "gy"), None)
    return jax.shard_map(
        per_device,
        mesh=mesh,
        in_specs=(rows, rows, rows, rows, P(("gx", "gy")), P()),
        out_specs=(rows, rows, rows),
        check_vma=False,
    )
```

time: 61.7 us -> 52.7 us (0.85)
  local copies, waits for them, and re-layouts: 6.56 us -> 0 us
  Pallas kernels: 54.2 us -> 51.9 us
    unnamed x14 -> x0, local copies, waits for them, and re-layouts: 6.55 us -> none
    pallas_call x1 -> x2, Pallas kernels: 54.2 us -> 51.9 us  [the longest x1 51 us: per_device(): pl.pallas_call(kernel, out_shape=(out, out, out), in_specs=[hbm] * 6, out...]
where the time goes in v2:
time: 52.7 us; the launch traced here: 52.6 us
  Pallas kernels  51.9 us (98%)
  between operations  0.64 us (1%)
    pallas_call x1, Pallas kernels, per_device(): pl.pallas_call(kernel, out_shape=(out, out, out), in_specs=[hbm] * 6, out...  51 us

profile of v2, /device:TPU:1, one launch (start us, length us, event | category | flops | bytes accessed | tf_op | source)
XLA Modules:
  0.0 52.6 jit_solution(6407198526292504373)
XLA Ops:
  0.6 51.0 %shard_map.85 = (bf16[128,1024]{1,0:T(8,128)(2,1)S(1)}, bf16[128,1024]{1,0:T(8,128)(2,1)S(1)}, bf16[128,1024]{1,0:T(8,128)(2,1)S(1)}) custom-call(bf16[128,1024]{1,0:T(8,128)(2,1)} %q_hbm.1, bf16[128,1024]{1,0:T(8,128)(2,1)} %k_hbm.1, bf16[128,1024]{1,0:T(8,128)(2,1)} %v_hbm.1, bf16[128,1024]{1,0:T(8,128)(2,1)} %g_hbm.1, s32[1,128]{1,0:T(1,128)} %bitcast.3, ...), custom_call_target="tpu_custom_call" | custom-call | tf_op jit(solution)/shard_map/pallas_call | solution.py:426
  51.7 0.9 %shard_map.86 = (bf16[128,1024]{1,0:T(8,128)(2,1)}, bf16[128,1024]{1,0:T(8,128)(2,1)}, bf16[128,1024]{1,0:T(8,128)(2,1)}) custom-call(bf16[128,1024]{1,0:T(8,128)(2,1)S(1)} %get-tuple-element.6.qi, bf16[128,1024]{1,0:T(8,128)(2,1)S(1)} %get-tuple-element.7.ki, bf16[128,1024]{1,0:T(8,128)(2,1)S(1)} %get-tuple-element.8.vi), custom_call_target="tpu_custom_call" | custom-call | tf_op jit(solution)/shard_map/pallas_call | solution.py:461

commit v3 on v2

--- a/solution.py
+++ b/solution.py
@@ -32,12 +32,10 @@
     return mm(a, b, 0, 0)
 
 
-def kernel(
+def exchange(
     q_hbm, k_hbm, v_hbm, g_hbm, cls_hbm, tab_hbm,
-    qo_ref, ko_ref, vo_ref,
-    q_ref, k_ref, v_ref, g_ref, cls_ref, tab_ref,
-    gates, hg, lev_ref, st_send, qb, gb, sb, gtb, lacc, qloc, kloc, vloc,
-    lbuf, urecv, bsend, brecv, ysum, vsend, wsend, xsend, rbuf, ctr, dacc, csend, dsend, crecv, drecv,
+    qb, gb, sb, gtb, lbuf, k_ref, v_ref, qloc, kloc, vloc,
+    q_ref, g_ref, cls_ref, tab_ref, gates, hg, lev_ref, st_send, lacc,
     lsem, ssem, rsem,
 ):
     gx = lax.axis_index("gx")
@@ -63,9 +61,8 @@
         return (r * 2 + core, gy)
 
     barrier = pltpu.get_barrier_semaphore()
-    for i in range(7):
-        for dev in (dev_p(near[i]), dev_a(far[i]), dev_y((y + i + 1) % 8)):
-            pl.semaphore_signal(barrier, inc=1, device_id=dev, device_id_type=MESH)
+    for r in near:
+        pl.semaphore_signal(barrier, inc=1, device_id=dev_p(r), device_id_type=MESH)
 
     loads = []
     for i, (src, dst) in enumerate((
@@ -89,10 +86,6 @@
                 like = qb.at[0]
             elif kind == KT:
                 like = gtb.at[0]
-            elif kind == KB:
-                like = brecv.at[0]
-            else:
-                like = urecv.at[0, 0]
             pltpu.make_async_copy(like, like, ssem.at[kind, i]).wait()
 
     def local(kind, src, dst, slot):
@@ -107,11 +100,6 @@
     def rows16(r):
         return pl.ds(pl.multiple_of(r * 16, 16), 16)
 
-    zero = jnp.zeros((16, N), F32)
-    for l in range(3, 9):
-        @pl.when(flag[l] == 0)
-        def _():
-            rbuf[l - 3] = jnp.zeros((N, N), BF16)
     loads[0].wait()
     loads[1].wait()
     classes = lax.broadcasted_iota(jnp.int32, (32, N), 0)
@@ -126,7 +114,7 @@
     loads[2].wait()
     loads[3].wait()
 
-    pl.semaphore_wait(barrier, 21)
+    pl.semaphore_wait(barrier, 7)
 
     for i, r in enumerate(near):
         send(KQ, i, cols(q_ref, r), qb.at[p], p, dev_p(r))
@@ -171,7 +159,7 @@
         qloc[:, c] = tn(wg, k)
         return 0
 
-    lax.fori_loop(0, 4, own_head, 0)
+    lax.fori_loop(0, HEADS, own_head, 0)
 
     for i, r in enumerate([p] + near):
         arrived(KQ, qb.at[r], r)
@@ -186,94 +174,102 @@
         elif i < 7:
             lacc[...] += part
         else:
-            lbuf[1:7] = (lacc[...] + part).astype(BF16).reshape(6, N, N)
+            lbuf[...] = (lacc[...] + part).astype(BF16).reshape(6, N, N)
+    for r in range(8):
+        arrived(KS, sb.at[r], r)
+    sent(sends)
+
+
+def combine(
+    qb, gb, sb, gtb, lbuf, k_ref, v_ref, qloc, kloc, vloc,
+    qo_ref, ko_ref, vo_ref,
+    tsend, urecv, bsend, brecv, ysum, vsend, wsend, xsend, rbuf, ctr, dacc, csend, dsend, crecv, drecv,
+    ssem, rsem,
+):
+    gx = lax.axis_index("gx")
+    gy = lax.axis_index("gy")
+    y = gx // 2
+    core = gx % 2
+    zz = gy // 8
+    p = gy % 8
+    z0 = p // 4
+    x = p % 4
+    a = core * 4 + zz
+    flag = {3: zz % 2, 4: zz // 2, 5: core, 6: y % 2, 7: y // 2 % 2, 8: y // 4}
+    near = [(z0 + dz) % 2 * 4 + (x + dx) % 4 for dz, dx in NEAR]
+    far = [(core + dc) % 2 * 4 + (zz + dz) % 4 for dc, dz in FAR]
+
+    def dev_p(r):
+        return (gx, zz * 8 + r)
+
+    def dev_a(r):
+        return (y * 2 + r // 4, (r % 4) * 8 + p)
+
+    def dev_y(r):
+        return (r * 2 + core, gy)
+
+    barrier = pltpu.get_barrier_semaphore()
+    for i in range(7):
+        for dev in (dev_a(far[i]), dev_y((y + i + 1) % 8), dev_p(near[i])):
+            pl.semaphore_signal(barrier, inc=1, device_id=dev, device_id_type=MESH)
+
+    sends = []
+
+    def send(kind, i, src, dst, slot, dev, keep=sends):
+        pltpu.make_async_remote_copy(
+            src_ref=src, dst_ref=dst, send_sem=ssem.at[kind, i], recv_sem=rsem.at[kind, slot],
+            device_id=dev, device_id_type=MESH,
+        ).start()
+        keep.append((kind, i))
+
+    def sent(done):
+        for kind, i in done:
+            if kind >= KC:
+                like = csend.at[0]
+            elif kind == KB:
+                like = brecv.at[0]
+            else:
+                like = urecv.at[0, 0]
+            pltpu.make_async_copy(like, like, ssem.at[kind, i]).wait()
+
+    def local(kind, src, dst, slot):
+        pltpu.make_async_copy(src, dst, rsem.at[kind, slot]).start()
+
+    def arrived(kind, dst, slot):
+        pltpu.make_async_copy(dst, dst, rsem.at[kind, slot]).wait()
+
+    def cols(ref, r):
+        return ref.at[:, pl.ds(pl.multiple_of(r * N, N), N)]
+
+    def rows16(r):
+        return pl.ds(pl.multiple_of(r * 16, 16), 16)
+
+    zero = jnp.zeros((16, N), F32)
+    for l in range(3, 9):
+        @pl.when(flag[l] == 0)
+        def _():
+            rbuf[l - 3] = jnp.zeros((N, N), BF16)
+    states = []
+    for r in range(8):
+        states.append(sb[r].astype(F32))
+    pair = [states[2 * j] + states[2 * j + 1] for j in range(4)]
+    quad = [pair[0] + pair[1], pair[2] + pair[3]]
+    tsend[...] = (quad[0] + quad[1]).astype(BF16)
+    pl.semaphore_wait(barrier, 21)
+
     kept = {}
     for l in range(8, 2, -1):
         kept[l] = []
         @pl.when(flag[l] == 1)
         def _():
             for i, r in enumerate(far):
-                send(KL + l - 3, i, lbuf.at[l - 2, rows16(r), :], urecv.at[a, l - 2], a, dev_a(r), kept[l])
-            local(KL + l - 3, lbuf.at[l - 2, rows16(a), :], urecv.at[a, l - 2], a)
-
-    states = []
-    for r in range(8):
-        arrived(KS, sb.at[r], r)
-        states.append(sb[r].astype(F32))
-    pair = [states[2 * j] + states[2 * j + 1] for j in range(4)]
-    quad = [pair[0] + pair[1], pair[2] + pair[3]]
-    lbuf[0] = (quad[0] + quad[1]).astype(BF16)
+                send(KL + l - 3, i, lbuf.at[l - 3, rows16(r), :], urecv.at[a, l - 2], a, dev_a(r), kept[l])
+            local(KL + l - 3, lbuf.at[l - 3, rows16(a), :], urecv.at[a, l - 2], a)
+
     for i, r in enumerate(far):
-        send(KU, i, lbuf.at[0, rows16(r), :], urecv.at[a, 0], a, dev_a(r))
-    local(KU, lbuf.at[0, rows16(a), :], urecv.at[a, 0], a)
-
-    lax.fori_loop(4, HEADS, own_head, 0)
-
-    lows = {}
-    for l in range(3, 6):
-        for r in range(8):
-            if r >> (l - 3) & 1:
-                arrived(KL + l - 3, urecv.at[r, l - 2], r)
-                lows[l, r] = urecv[r, l - 2].astype(F32)
-    for l in range(6, 9):
-        @pl.when(flag[l] == 1)
-        def _():
-            total = zero
-            for r in range(8):
-                arrived(KL + l - 3, urecv.at[r, l - 2], r)
-                total = total + urecv[r, l - 2].astype(F32)
-            bsend[l - 5] = total
-    down = []
-    for r in range(8):
-        down.append([])
-        @pl.when(r < y)
-        def _():
-            high = jnp.where(y // 4 != r // 4, 3, jnp.where(y // 2 != r // 2, 2, 1))
-            send(KB, r, bsend.at[high], brecv.at[y], y, dev_y(r), down[r])
-    l4 = {3: lows[4, 2] + lows[4, 3], 7: lows[4, 6] + lows[4, 7]}
-    l5 = (lows[5, 4] + lows[5, 5]) + (lows[5, 6] + lows[5, 7])
-    dmid = []
-    for r in range(8):
-        acc = zero
-        if not r & 1:
-            acc = acc + lows[3, r + 1]
-        if not r & 2:
-            acc = acc + l4[r | 3]
-        if not r & 4:
-            acc = acc + l5
-        dmid.append(acc)
-
-    tops = []
-    for r in range(8):
-        arrived(KU, urecv.at[r, 0], r)
-        tops.append(urecv[r, 0].astype(F32))
-    tpair = [tops[2 * j] + tops[2 * j + 1] for j in range(4)]
-    tquad = [tpair[0] + tpair[1], tpair[2] + tpair[3]]
-    bsend[0] = tquad[0] + tquad[1]
-    up = []
-    for r in range(8):
-        up.append([])
-        @pl.when(r > y)
-        def _():
-            send(KB, r, bsend.at[0], brecv.at[y], y, dev_y(r), up[r])
-    for r in range(8):
-        if r & 1:
-            vsend[r, 0] = tops[r - 1].astype(BF16)
-        if r & 2:
-            vsend[r, 1] = tpair[(r >> 1) ^ 1].astype(BF16)
-        if r & 4:
-            vsend[r, 2] = tquad[0].astype(BF16)
-    side = {}
-    for i, r in enumerate(far):
-        for l in range(3):
-            side[i, l] = []
-            @pl.when(r // 2**l % 2 == 1)
-            def _():
-                send(KV + l, i, vsend.at[r, l], rbuf.at[l, rows16(a), :], a, dev_a(r), side[i, l])
-    for l in range(3):
-        @pl.when(flag[3 + l] == 1)
-        def _():
-            local(KV + l, vsend.at[a, l], rbuf.at[l, rows16(a), :], a)
+        send(KU, i, tsend.at[rows16(r), :], urecv.at[a, 0], a, dev_a(r))
+    local(KU, tsend.at[rows16(a), :], urecv.at[a, 0], a)
+
 
     low = {}
     for r in range(1, 8):
@@ -306,6 +302,72 @@
                 acc = acc + rows[l : l + 1, :] * nt(left, gb[b])
         ctr[b] = acc
 
+    lows = {}
+    for l in range(3, 6):
+        for r in range(8):
+            if r >> (l - 3) & 1:
+                arrived(KL + l - 3, urecv.at[r, l - 2], r)
+                lows[l, r] = urecv[r, l - 2].astype(F32)
+    for l in range(6, 9):
+        @pl.when(flag[l] == 1)
+        def _():
+            total = zero
+            for r in range(8):
+                arrived(KL + l - 3, urecv.at[r, l - 2], r)
+                total = total + urecv[r, l - 2].astype(F32)
+            bsend[l - 5] = total
+    down = []
+    for r in range(8):
+        down.append([])
+        @pl.when(r < y)
+        def _():
+            high = jnp.where(y // 4 != r // 4, 3, jnp.where(y // 2 != r // 2, 2, 1))
+            send(KB, r, bsend.at[high], brecv.at[y], y, dev_y(r), down[r])
+    l4 = {3: lows[4, 2] + lows[4, 3], 7: lows[4, 6] + lows[4, 7]}
+    l5 = (lows[5, 4] + lows[5, 5]) + (lows[5, 6] + lows[5, 7])
+    dmid = []
+    for r in range(8):
+        acc = zero
+        if not r & 1:
+            acc = acc + lows[3, r + 1]
+        if not r & 2:
+            acc = acc + l4[r | 3]
+        if not r & 4:
+            acc = acc + l5
+        dmid.append(acc)
+
+    tops = []
+    for r in range(8):
+        arrived(KU, urecv.at[r, 0], r)
+        tops.append(urecv[r, 0].astype(F32))
+    tpair = [tops[2 * j] + tops[2 * j + 1] for j in range(4)]
+    tquad = [tpair[0] + tpair[1], tpair[2] + tpair[3]]
+    bsend[0] = tquad[0] + tquad[1]
+    up = []
+    for r in range(8):
+        up.append([])
+        @pl.when(r > y)
+        def _():
+            send(KB, r, bsend.at[0], brecv.at[y], y, dev_y(r), up[r])
+    for r in range(8):
+        if r & 1:
+            vsend[r, 0] = tops[r - 1].astype(BF16)
+        if r & 2:
+            vsend[r, 1] = tpair[(r >> 1) ^ 1].astype(BF16)
+        if r & 4:
+            vsend[r, 2] = tquad[0].astype(BF16)
+    side = {}
+    for i, r in enumerate(far):
+        for l in range(3):
+            side[i, l] = []
+            @pl.when(r // 2**l % 2 == 1)
+            def _():
+                send(KV + l, i, vsend.at[r, l], rbuf.at[l, rows16(a), :], a, dev_a(r), side[i, l])
+    for l in range(3):
+        @pl.when(flag[3 + l] == 1)
+        def _():
+            local(KV + l, vsend.at[a, l], rbuf.at[l, rows16(a), :], a)
+
     ysum[...] = jnp.zeros((4, 16, N), F32)
     for r in range(1, 8):
         @pl.when(r > y)
@@ -418,28 +480,45 @@
 def per_device(query_rows, key_rows, value_rows, out_grad, gate_class, gate_table):
     table = gate_table.transpose(1, 2, 0)
     out = jax.ShapeDtypeStruct((N, HEADS * N), BF16)
+    loc = jax.ShapeDtypeStruct((N, HEADS * N), F32)
+    eight = jax.ShapeDtypeStruct((8, N, N), BF16)
     vmem = pl.BlockSpec(memory_space=pltpu.VMEM)
     hbm = pl.BlockSpec(memory_space=pltpu.HBM)
     cube = lambda n, dtype: pltpu.VMEM((n, N, N), dtype)
-    wide = pltpu.VMEM((N, HEADS * N), F32)
     flat = pltpu.VMEM((N, HEADS * N), BF16)
-    outs = pl.pallas_call(
-        kernel,
-        out_shape=(out, out, out),
+    args = (query_rows, key_rows, value_rows, out_grad, gate_class.reshape(1, N), table)
+    held = pl.pallas_call(
+        exchange,
+        out_shape=(
+            eight, eight, eight, jax.ShapeDtypeStruct((8, 16, N), F32),
+            jax.ShapeDtypeStruct((6, N, N), BF16), out, out, loc, loc, loc,
+        ),
         in_specs=[hbm] * 6,
-        out_specs=(vmem, vmem, vmem),
+        out_specs=(vmem,) * 10,
         scratch_shapes=[
-            flat, flat, flat, flat,
+            flat, flat,
             pltpu.VMEM((1, N), jnp.int32),
             pltpu.VMEM((20, HEADS, 32), F32),
             pltpu.VMEM((20 * HEADS, N), F32),
             pltpu.VMEM((HEADS, 24, N), F32),
             pltpu.VMEM((N, N), jnp.int32),
-            cube(8, BF16), cube(8, BF16), cube(8, BF16), cube(8, BF16),
-            pltpu.VMEM((8, 16, N), F32),
+            cube(8, BF16),
             pltpu.VMEM((6 * N, N), F32),
-            wide, wide, wide,
-            cube(7, BF16),
+            pltpu.SemaphoreType.DMA((6,)),
+            pltpu.SemaphoreType.DMA((4, 8)),
+            pltpu.SemaphoreType.DMA((4, 8)),
+        ],
+        compiler_params=pltpu.CompilerParams(
+            collective_id=0, has_side_effects=True, vmem_limit_bytes=24 * 1024 * 1024
+        ),
+    )(*[pltpu.with_memory_space_constraint(one, pltpu.HBM) for one in args])
+    outs = pl.pallas_call(
+        combine,
+        out_shape=(out, out, out),
+        in_specs=[vmem] * 10,
+        out_specs=(vmem, vmem, vmem),
+        scratch_shapes=[
+            pltpu.VMEM((N, N), BF16),
             pltpu.VMEM((8, 7, 16, N), BF16),
             pltpu.VMEM((4, 16, N), F32),
             pltpu.VMEM((8, 16, N), F32),
@@ -450,14 +529,13 @@
             cube(7, BF16),
             cube(8, F32), cube(8, F32),
             cube(8, BF16), cube(8, BF16), cube(8, BF16), cube(8, BF16),
-            pltpu.SemaphoreType.DMA((6,)),
             pltpu.SemaphoreType.DMA((KINDS, 8)),
             pltpu.SemaphoreType.DMA((KINDS, 8)),
         ],
         compiler_params=pltpu.CompilerParams(
-            collective_id=0, has_side_effects=True, vmem_limit_bytes=40 * 1024 * 1024
+            collective_id=1, has_side_effects=True, vmem_limit_bytes=24 * 1024 * 1024
         ),
-    )(*[pltpu.with_memory_space_constraint(one, pltpu.HBM) for one in (query_rows, key_rows, value_rows, out_grad, gate_class.reshape(1, N), table)])
+    )(*held)
     return pl.pallas_call(
         write_out,
         out_shape=(out, out, out),

time: 52.7 us -> 59.2 us (1.12)
  Pallas kernels: 51.9 us -> 58.4 us
    pallas_call x1 -> x2, Pallas kernels: 51 us -> 57.5 us  [the longest x1 43.9 us: per_device(): pl.pallas_call(combine, out_shape=(out, out, out), in_specs=[vmem] * 10,...]
where the time goes in v3:
time: 59.2 us; the launch traced here: 59 us
  Pallas kernels  58.4 us (99%)
  between operations  0.65 us (1%)
    pallas_call x1, Pallas kernels, per_device(): pl.pallas_call(combine, out_shape=(out, out, out), in_specs=[vmem] * 10,...  43.9 us
    pallas_call x1, Pallas kernels, per_device(): pl.pallas_call(exchange, out_shape=(eight, eight, eight, jax.ShapeDtypeSt...  13.6 us

profile of v3, /device:TPU:1, one launch (start us, length us, event | category | flops | bytes accessed | tf_op | source)
XLA Modules:
  0.0 59.0 jit_solution(10138513048671864902)
XLA Ops:
  0.6 13.6 %shard_map.85 = (bf16[8,128,128]{2,1,0:T(8,128)(2,1)S(1)}, bf16[8,128,128]{2,1,0:T(8,128)(2,1)S(1)}, bf16[8,128,128]{2,1,0:T(8,128)(2,1)S(1)}, f32[8,16,128]{2,1...) custom-call(bf16[128,1024]{1,0:T(8,128)(2,1)} %q_hbm.1, ...), custom_call_target="tpu_custom_call" | custom-call | tf_op jit(solution)/shard_map/pallas_call | solution.py:490
  14.2 43.9 %shard_map.86 = (bf16[128,1024]{1,0:T(8,128)(2,1)S(1)}, bf16[128,1024]{1,0:T(8,128)(2,1)S(1)}, bf16[128,1024]{1,0:T(8,128)(2,1)S(1)}) custom-call(bf16[8,128,128]{2,1,0:T(8,128)(2,1)S(1)} %get-tuple-element.16.qb, bf16[8,128,128]{2,1,0:T(8,128)(2,1)S(1)} %get-tuple-element.17.gb, bf16[8,128,128]{2,1,0:T(8,128)(2,1)S(1)} %get-tuple-element.18.sb, ...), custom_call_target="tpu_custom_call" | custom-call | tf_op jit(solution)/shard_map/pallas_call | solution.py:515
  58.1 0.9 %shard_map.87 = (bf16[128,1024]{1,0:T(8,128)(2,1)}, bf16[128,1024]{1,0:T(8,128)(2,1)}, bf16[128,1024]{1,0:T(8,128)(2,1)}) custom-call(bf16[128,1024]{1,0:T(8,128)(2,1)S(1)} %get-tuple-element.26.qi, bf16[128,1024]{1,0:T(8,128)(2,1)S(1)} %get-tuple-element.27.ki, bf16[128,1024]{1,0:T(8,128)(2,1)S(1)} %get-tuple-element.28.vi), custom_call_target="tpu_custom_call" | custom-call | tf_op jit(solution)/shard_map/pallas_call | solution.py:539

commit v4 on v2

--- a/solution.py
+++ b/solution.py
@@ -11,7 +11,8 @@
 N = 128
 HEADS = 8
 KQ, KG, KT, KS, KL, KU, KB, KV, KW, KX, KC, KD = 0, 1, 2, 3, 4, 10, 11, 12, 15, 16, 19, 20
-KINDS = 21
+KH = 21
+KINDS = 22
 NEAR = ((0, 1), (0, 3), (1, 0), (1, 1), (1, 3), (0, 2), (1, 2))
 FAR = ((0, 2), (1, 2), (0, 1), (0, 3), (1, 1), (1, 3), (1, 0))
 
@@ -36,8 +37,8 @@
     q_hbm, k_hbm, v_hbm, g_hbm, cls_hbm, tab_hbm,
     qo_ref, ko_ref, vo_ref,
     q_ref, k_ref, v_ref, g_ref, cls_ref, tab_ref,
-    gates, hg, lev_ref, st_send, qb, gb, sb, gtb, lacc, qloc, kloc, vloc,
-    lbuf, urecv, bsend, brecv, ysum, vsend, wsend, xsend, rbuf, ctr, dacc, csend, dsend, crecv, drecv,
+    gates, hg, lev_ref, st_send, qt_send, qb, gb, sb, gtb, lacc, qloc, kloc, vloc,
+    tsend, lbuf, urecv, bsend, brecv, ysum, vsend, wsend, xsend, rbuf, ctr, dacc, csend, dsend, crecv, drecv,
     lsem, ssem, rsem,
 ):
     gx = lax.axis_index("gx")
@@ -85,7 +86,9 @@
 
     def sent(done):
         for kind, i in done:
-            if kind < KL and kind != KT or kind >= KC:
+            if kind in (KQ, KH):
+                like = qb.at[0, pl.ds(0, 64)]
+            elif kind in (KG, KS, KC, KD):
                 like = qb.at[0]
             elif kind == KT:
                 like = gtb.at[0]
@@ -124,26 +127,29 @@
         hg[h, 0:20] = gates[pl.ds(h, 20, stride=HEADS), :]
         hg[h, 20:24] = jnp.zeros((4, N), F32)
     loads[2].wait()
-    loads[3].wait()
-
-    pl.semaphore_wait(barrier, 21)
-
-    for i, r in enumerate(near):
-        send(KQ, i, cols(q_ref, r), qb.at[p], p, dev_p(r))
-        send(KG, i, cols(g_ref, r), gb.at[p], p, dev_p(r))
-        send(KT, i, hg.at[r, pl.ds(8, 16)], gtb.at[p], p, dev_p(r))
-    local(KQ, cols(q_ref, p), qb.at[p], p)
-    local(KG, cols(g_ref, p), gb.at[p], p)
-    local(KT, hg.at[p, pl.ds(8, 16)], gtb.at[p], p)
-
     loads[4].wait()
     loads[5].wait()
     for h in range(HEADS):
         c = slice(h * N, h * N + N)
         st_send[h] = tn(k_ref[:, c], v_ref[:, c]).astype(BF16)
+        qt_send[h] = q_ref[:, c].T
+    loads[3].wait()
+
+    pl.semaphore_wait(barrier, 21)
+
+    half = (pl.ds(0, 64), pl.ds(64, 64))
     for i, r in enumerate(near):
         send(KS, i, st_send.at[r], sb.at[p], p, dev_p(r))
+    for i, r in enumerate(near):
+        send(KG, i, cols(g_ref, r), gb.at[p], p, dev_p(r))
+        send(KT, i, hg.at[r, pl.ds(8, 16)], gtb.at[p], p, dev_p(r))
+    for kind, part in ((KQ, half[0]), (KH, half[1])):
+        for i, r in enumerate(near):
+            send(kind, i, qt_send.at[r, part], qb.at[p, part], p, dev_p(r))
+        local(kind, qt_send.at[p, part], qb.at[p, part], p)
     local(KS, st_send.at[p], sb.at[p], p)
+    local(KG, cols(g_ref, p), gb.at[p], p)
+    local(KT, hg.at[p, pl.ds(8, 16)], gtb.at[p], p)
 
     s_id = lax.broadcasted_iota(jnp.int32, (N, N), 0)
     t_id = lax.broadcasted_iota(jnp.int32, (N, N), 1)
@@ -171,78 +177,50 @@
         qloc[:, c] = tn(wg, k)
         return 0
 
-    lax.fori_loop(0, 4, own_head, 0)
-
-    for i, r in enumerate([p] + near):
-        arrived(KQ, qb.at[r], r)
-        arrived(KG, gb.at[r], r)
-        arrived(KT, gtb.at[r], r)
-        qt = qb[r].T.astype(F32)
-        rows = gtb[r]
-        scaled = jnp.concatenate([(qt * rows[l : l + 1, :]).astype(BF16) for l in range(3, 9)], axis=0)
-        part = nn(scaled, gb[r])
-        if i == 0:
-            lacc[...] = part
-        elif i < 7:
-            lacc[...] += part
-        else:
-            lbuf[1:7] = (lacc[...] + part).astype(BF16).reshape(6, N, N)
-    kept = {}
-    for l in range(8, 2, -1):
-        kept[l] = []
-        @pl.when(flag[l] == 1)
-        def _():
-            for i, r in enumerate(far):
-                send(KL + l - 3, i, lbuf.at[l - 2, rows16(r), :], urecv.at[a, l - 2], a, dev_a(r), kept[l])
-            local(KL + l - 3, lbuf.at[l - 2, rows16(a), :], urecv.at[a, l - 2], a)
+    lax.fori_loop(0, HEADS, own_head, 0)
 
     states = []
     for r in range(8):
         arrived(KS, sb.at[r], r)
         states.append(sb[r].astype(F32))
     pair = [states[2 * j] + states[2 * j + 1] for j in range(4)]
-    quad = [pair[0] + pair[1], pair[2] + pair[3]]
-    lbuf[0] = (quad[0] + quad[1]).astype(BF16)
+    tsend[...] = ((pair[0] + pair[1]) + (pair[2] + pair[3])).astype(BF16)
     for i, r in enumerate(far):
-        send(KU, i, lbuf.at[0, rows16(r), :], urecv.at[a, 0], a, dev_a(r))
-    local(KU, lbuf.at[0, rows16(a), :], urecv.at[a, 0], a)
-
-    lax.fori_loop(4, HEADS, own_head, 0)
-
-    lows = {}
-    for l in range(3, 6):
-        for r in range(8):
-            if r >> (l - 3) & 1:
-                arrived(KL + l - 3, urecv.at[r, l - 2], r)
-                lows[l, r] = urecv[r, l - 2].astype(F32)
-    for l in range(6, 9):
-        @pl.when(flag[l] == 1)
-        def _():
-            total = zero
-            for r in range(8):
-                arrived(KL + l - 3, urecv.at[r, l - 2], r)
-                total = total + urecv[r, l - 2].astype(F32)
-            bsend[l - 5] = total
-    down = []
-    for r in range(8):
-        down.append([])
-        @pl.when(r < y)
-        def _():
-            high = jnp.where(y // 4 != r // 4, 3, jnp.where(y // 2 != r // 2, 2, 1))
-            send(KB, r, bsend.at[high], brecv.at[y], y, dev_y(r), down[r])
-    l4 = {3: lows[4, 2] + lows[4, 3], 7: lows[4, 6] + lows[4, 7]}
-    l5 = (lows[5, 4] + lows[5, 5]) + (lows[5, 6] + lows[5, 7])
-    dmid = []
-    for r in range(8):
-        acc = zero
-        if not r & 1:
-            acc = acc + lows[3, r + 1]
-        if not r & 2:
-            acc = acc + l4[r | 3]
-        if not r & 4:
-            acc = acc + l5
-        dmid.append(acc)
-
+        send(KU, i, tsend.at[rows16(r), :], urecv.at[a, 0], a, dev_a(r))
+    local(KU, tsend.at[rows16(a), :], urecv.at[a, 0], a)
+
+    for part in range(2):
+        for i, r in enumerate([p] + near):
+            if part == 0:
+                arrived(KG, gb.at[r], r)
+                arrived(KT, gtb.at[r], r)
+            arrived((KQ, KH)[part], qb.at[r, half[part]], r)
+            qt = qb[r, part * 64 : part * 64 + 64].astype(F32)
+            rows = gtb[r]
+            scaled = jnp.concatenate([(qt * rows[l : l + 1, :]).astype(BF16) for l in range(3, 9)], axis=0)
+            prod = nn(scaled, gb[r])
+            if i == 0:
+                lacc[...] = prod
+            elif i < 7:
+                lacc[...] += prod
+            else:
+                lbuf[:, part * 64 : part * 64 + 64] = (lacc[...] + prod).astype(BF16).reshape(6, 64, N)
+        for l in range(8, 2, -1):
+            @pl.when(flag[l] == 1)
+            def _():
+                for dz in (2, 1, 3):
+                    r = part * 4 + (zz + dz) % 4
+                    send(KL + l - 3, part * 4 + dz, lbuf.at[l - 3, rows16(r), :], urecv.at[a, l - 2], a, dev_a(r), [])
+                @pl.when(core == part)
+                def _():
+                    local(KL + l - 3, lbuf.at[l - 3, rows16(a), :], urecv.at[a, l - 2], a)
+                @pl.when(core != part)
+                def _():
+                    r = part * 4 + zz
+                    send(KL + l - 3, part * 4, lbuf.at[l - 3, rows16(r), :], urecv.at[a, l - 2], a, dev_a(r), [])
+    kept = {}
+
+    ysum[...] = jnp.zeros((4, 16, N), F32)
     tops = []
     for r in range(8):
         arrived(KU, urecv.at[r, 0], r)
@@ -277,7 +255,7 @@
 
     low = {}
     for r in range(1, 8):
-        qt = qb[r].T.astype(F32)
+        qt = qb[r].astype(F32)
         rows = gtb[r]
         for l in range(3):
             if r >> l & 1:
@@ -306,19 +284,6 @@
                 acc = acc + rows[l : l + 1, :] * nt(left, gb[b])
         ctr[b] = acc
 
-    ysum[...] = jnp.zeros((4, 16, N), F32)
-    for r in range(1, 8):
-        @pl.when(r > y)
-        def _():
-            arrived(KB, brecv.at[r], r)
-            ysum[3] += brecv[r]
-    dtop = ysum[3]
-    for r in range(8):
-        wsend[r] = (dmid[r] + dtop).astype(BF16)
-    for i, r in enumerate(far):
-        send(KW, i, wsend.at[r], rbuf.at[6, rows16(a), :], a, dev_a(r))
-    local(KW, wsend.at[a], rbuf.at[6, rows16(a), :], a)
-
     for r in range(7):
         @pl.when(r < y)
         def _():
@@ -335,6 +300,40 @@
                 send(KX + l, i, xsend.at[l], rbuf.at[3 + l, rows16(a), :], a, dev_a(r), kept[9 + l])
             local(KX + l, xsend.at[l], rbuf.at[3 + l, rows16(a), :], a)
 
+    lows = {}
+    for l in range(3, 6):
+        for r in range(8):
+            if r >> (l - 3) & 1:
+                arrived(KL + l - 3, urecv.at[r, l - 2], r)
+                lows[l, r] = urecv[r, l - 2].astype(F32)
+    for l in range(6, 9):
+        @pl.when(flag[l] == 1)
+        def _():
+            total = zero
+            for r in range(8):
+                arrived(KL + l - 3, urecv.at[r, l - 2], r)
+                total = total + urecv[r, l - 2].astype(F32)
+            bsend[l - 5] = total
+    down = []
+    for r in range(8):
+        down.append([])
+        @pl.when(r < y)
+        def _():
+            high = jnp.where(y // 4 != r // 4, 3, jnp.where(y // 2 != r // 2, 2, 1))
+            send(KB, r, bsend.at[high], brecv.at[y], y, dev_y(r), down[r])
+    l4 = {3: lows[4, 2] + lows[4, 3], 7: lows[4, 6] + lows[4, 7]}
+    l5 = (lows[5, 4] + lows[5, 5]) + (lows[5, 6] + lows[5, 7])
+    dmid = []
+    for r in range(8):
+        acc = zero
+        if not r & 1:
+            acc = acc + lows[3, r + 1]
+        if not r & 2:
+            acc = acc + l4[r | 3]
+        if not r & 4:
+            acc = acc + l5
+        dmid.append(acc)
+
     for l in range(3):
         @pl.when(flag[3 + l] == 1)
         def _():
@@ -352,13 +351,17 @@
 
     lax.fori_loop(0, 8, middle, 0, unroll=2)
 
-    for r in range(8):
-        arrived(KW, rbuf.at[6, pl.ds(16 * r, 16), :], r)
-    for b in range(8):
-        dsend[b] = (dacc[b] + rbuf[6].astype(F32)).astype(BF16)
-    for i, r in enumerate(near):
-        send(KD, i, dsend.at[r], drecv.at[p], p, dev_p(r))
-    local(KD, dsend.at[p], drecv.at[p], p)
+    for r in range(1, 8):
+        @pl.when(r > y)
+        def _():
+            arrived(KB, brecv.at[r], r)
+            ysum[3] += brecv[r]
+    dtop = ysum[3]
+    for r in range(8):
+        wsend[r] = (dmid[r] + dtop).astype(BF16)
+    for i, r in enumerate(far):
+        send(KW, i, wsend.at[r], rbuf.at[6, rows16(a), :], a, dev_a(r))
+    local(KW, wsend.at[a], rbuf.at[6, rows16(a), :], a)
 
     for l in range(3):
         @pl.when(flag[6 + l] == 1)
@@ -377,19 +380,36 @@
             send(KC, i, csend.at[b], crecv.at[p], p, dev_p(b))
     local(KC, csend.at[p], crecv.at[p], p)
 
-    for h in range(HEADS):
-        c = slice(h * N, h * N + N)
-        arrived(KD, drecv.at[h], h)
-        d = drecv[h]
+    for r in range(8):
+        arrived(KW, rbuf.at[6, pl.ds(16 * r, 16), :], r)
+    dall = rbuf[6].astype(F32)
+    for i, r in enumerate(near):
+        dsend[r] = (dacc[r] + dall).astype(BF16)
+        send(KD, i, dsend.at[r], drecv.at[p], p, dev_p(r))
+    dsend[p] = (dacc[p] + dall).astype(BF16)
+    local(KD, dsend.at[p], drecv.at[p], p)
+
+    for r in [p] + near:
+        c = pl.ds(pl.multiple_of(r * N, N), N)
+        arrived(KC, crecv.at[r], r)
+        qo_ref[:, c] = (qloc[:, c] + crecv[r].astype(F32)).astype(BF16)
+    for r in [p] + near:
+        c = pl.ds(pl.multiple_of(r * N, N), N)
+        arrived(KD, drecv.at[r], r)
+        d = drecv[r]
         ko_ref[:, c] = (kloc[:, c] + nt(v_ref[:, c], d)).astype(BF16)
         vo_ref[:, c] = (vloc[:, c] + nn(k_ref[:, c], d)).astype(BF16)
-    for h in range(HEADS):
-        c = slice(h * N, h * N + N)
-        arrived(KC, crecv.at[h], h)
-        qo_ref[:, c] = (qloc[:, c] + crecv[h].astype(F32)).astype(BF16)
 
     sent(sends)
-    for l in range(3, 12):
+    for part in range(2):
+        for l in range(3, 9):
+            @pl.when(flag[l] == 1)
+            def _():
+                sent([(KL + l - 3, part * 4 + dz) for dz in (1, 2, 3)])
+                @pl.when(core != part)
+                def _():
+                    sent([(KL + l - 3, part * 4)])
+    for l in range(9, 12):
         @pl.when(flag[l if l < 9 else l - 3] == 1)
         def _():
             sent(kept[l])
@@ -435,11 +455,12 @@
             pltpu.VMEM((20 * HEADS, N), F32),
             pltpu.VMEM((HEADS, 24, N), F32),
             pltpu.VMEM((N, N), jnp.int32),
-            cube(8, BF16), cube(8, BF16), cube(8, BF16), cube(8, BF16),
+            cube(8, BF16), cube(8, BF16), cube(8, BF16), cube(8, BF16), cube(8, BF16),
             pltpu.VMEM((8, 16, N), F32),
-            pltpu.VMEM((6 * N, N), F32),
+            pltpu.VMEM((3 * N, N), F32),
             wide, wide, wide,
-            cube(7, BF16),
+            pltpu.VMEM((N, N), BF16),
+            cube(6, BF16),
             pltpu.VMEM((8, 7, 16, N), BF16),
             pltpu.VMEM((4, 16, N), F32),
             pltpu.VMEM((8, 16, N), F32),

time: 52.7 us -> 53.7 us (1.019)
  Pallas kernels: 51.9 us -> 52.9 us
    pallas_call x1, Pallas kernels: 51 us -> 52 us  [per_device(): pl.pallas_call(kernel, out_shape=(out, out, out), in_specs=[hbm] * 6, out...]
where the time goes in v4:
time: 53.7 us; the launch traced here: 53.6 us
  Pallas kernels  52.9 us (99%)
  between operations  0.64 us (1%)
    pallas_call x1, Pallas kernels, per_device(): pl.pallas_call(kernel, out_shape=(out, out, out), in_specs=[hbm] * 6, out...  52 us

profile of v4, /device:TPU:1, one launch (start us, length us, event | category | flops | bytes accessed | tf_op | source)
XLA Modules:
  0.0 53.6 jit_solution(15501400228196658757)
XLA Ops:
  0.6 52.0 %shard_map.85 = (bf16[128,1024]{1,0:T(8,128)(2,1)S(1)}, bf16[128,1024]{1,0:T(8,128)(2,1)S(1)}, bf16[128,1024]{1,0:T(8,128)(2,1)S(1)}) custom-call(bf16[128,1024]{1,0:T(8,128)(2,1)} %q_hbm.1, bf16[128,1024]{1,0:T(8,128)(2,1)} %k_hbm.1, bf16[128,1024]{1,0:T(8,128)(2,1)} %v_hbm.1, bf16[128,1024]{1,0:T(8,128)(2,1)} %g_hbm.1, s32[1,128]{1,0:T(1,128)} %bitcast.3, ...), custom_call_target="tpu_custom_call" | custom-call | tf_op jit(solution)/shard_map/pallas_call | solution.py:446
  52.6 0.9 %shard_map.86 = (bf16[128,1024]{1,0:T(8,128)(2,1)}, bf16[128,1024]{1,0:T(8,128)(2,1)}, bf16[128,1024]{1,0:T(8,128)(2,1)}) custom-call(bf16[128,1024]{1,0:T(8,128)(2,1)S(1)} %get-tuple-element.6.qi, bf16[128,1024]{1,0:T(8,128)(2,1)S(1)} %get-tuple-element.7.ki, bf16[128,1024]{1,0:T(8,128)(2,1)S(1)} %get-tuple-element.8.vi), custom_call_target="tpu_custom_call" | custom-call | tf_op jit(solution)/shard_map/pallas_call | solution.py:482

commit v5 on v4

--- a/solution.py
+++ b/solution.py
@@ -10,9 +10,8 @@
 BF16 = jnp.bfloat16
 N = 128
 HEADS = 8
-KQ, KG, KT, KS, KL, KU, KB, KV, KW, KX, KC, KD = 0, 1, 2, 3, 4, 10, 11, 12, 15, 16, 19, 20
-KH = 21
-KINDS = 22
+KS, KG, KT, KQ, KH, KU, KL, KB, KV, KX, KW, KC, KD = range(13)
+KINDS = 13
 NEAR = ((0, 1), (0, 3), (1, 0), (1, 1), (1, 3), (0, 2), (1, 2))
 FAR = ((0, 2), (1, 2), (0, 1), (0, 3), (1, 1), (1, 3), (1, 0))
 
@@ -38,7 +37,7 @@
     qo_ref, ko_ref, vo_ref,
     q_ref, k_ref, v_ref, g_ref, cls_ref, tab_ref,
     gates, hg, lev_ref, st_send, qt_send, qb, gb, sb, gtb, lacc, qloc, kloc, vloc,
-    tsend, lbuf, urecv, bsend, brecv, ysum, vsend, wsend, xsend, rbuf, ctr, dacc, csend, dsend, crecv, drecv,
+    tsend, lbuf, trecv, lrecv, bsend, brecv, ysum, vsend, wsend, xsend, rbuf, ctr, dacc, csend, dsend, crecv, drecv,
     lsem, ssem, rsem,
 ):
     gx = lax.axis_index("gx")
@@ -50,7 +49,6 @@
     z0 = p // 4
     x = p % 4
     a = core * 4 + zz
-    flag = {3: zz % 2, 4: zz // 2, 5: core, 6: y % 2, 7: y // 2 % 2, 8: y // 4}
     near = [(z0 + dz) % 2 * 4 + (x + dx) % 4 for dz, dx in NEAR]
     far = [(core + dc) % 2 * 4 + (zz + dz) % 4 for dc, dz in FAR]
 
@@ -75,28 +73,14 @@
         loads.append(pltpu.make_async_copy(src, dst, lsem.at[i]))
         loads[-1].start()
 
-    sends = []
-
-    def send(kind, i, src, dst, slot, dev, keep=sends):
+    def send(kind, src, dst, slot, dev):
         pltpu.make_async_remote_copy(
-            src_ref=src, dst_ref=dst, send_sem=ssem.at[kind, i], recv_sem=rsem.at[kind, slot],
+            src_ref=src, dst_ref=dst, send_sem=ssem.at[kind], recv_sem=rsem.at[kind, slot],
             device_id=dev, device_id_type=MESH,
         ).start()
-        keep.append((kind, i))
-
-    def sent(done):
-        for kind, i in done:
-            if kind in (KQ, KH):
-                like = qb.at[0, pl.ds(0, 64)]
-            elif kind in (KG, KS, KC, KD):
-                like = qb.at[0]
-            elif kind == KT:
-                like = gtb.at[0]
-            elif kind == KB:
-                like = brecv.at[0]
-            else:
-                like = urecv.at[0, 0]
-            pltpu.make_async_copy(like, like, ssem.at[kind, i]).wait()
+
+    def sent(kind, like):
+        pltpu.make_async_copy(like, like, ssem.at[kind]).wait()
 
     def local(kind, src, dst, slot):
         pltpu.make_async_copy(src, dst, rsem.at[kind, slot]).start()
@@ -111,10 +95,6 @@
         return pl.ds(pl.multiple_of(r * 16, 16), 16)
 
     zero = jnp.zeros((16, N), F32)
-    for l in range(3, 9):
-        @pl.when(flag[l] == 0)
-        def _():
-            rbuf[l - 3] = jnp.zeros((N, N), BF16)
     loads[0].wait()
     loads[1].wait()
     classes = lax.broadcasted_iota(jnp.int32, (32, N), 0)
@@ -138,18 +118,18 @@
     pl.semaphore_wait(barrier, 21)
 
     half = (pl.ds(0, 64), pl.ds(64, 64))
-    for i, r in enumerate(near):
-        send(KS, i, st_send.at[r], sb.at[p], p, dev_p(r))
-    for i, r in enumerate(near):
-        send(KG, i, cols(g_ref, r), gb.at[p], p, dev_p(r))
-        send(KT, i, hg.at[r, pl.ds(8, 16)], gtb.at[p], p, dev_p(r))
+    for r in near:
+        send(KS, st_send.at[r], sb.at[p], 0, dev_p(r))
+    for r in near:
+        send(KG, cols(g_ref, r), gb.at[p], p, dev_p(r))
+        send(KT, hg.at[r, pl.ds(8, 16)], gtb.at[p], 0, dev_p(r))
     for kind, part in ((KQ, half[0]), (KH, half[1])):
-        for i, r in enumerate(near):
-            send(kind, i, qt_send.at[r, part], qb.at[p, part], p, dev_p(r))
+        for r in near:
+            send(kind, qt_send.at[r, part], qb.at[p, part], p, dev_p(r))
         local(kind, qt_send.at[p, part], qb.at[p, part], p)
-    local(KS, st_send.at[p], sb.at[p], p)
+    local(KS, st_send.at[p], sb.at[p], 0)
     local(KG, cols(g_ref, p), gb.at[p], p)
-    local(KT, hg.at[p, pl.ds(8, 16)], gtb.at[p], p)
+    local(KT, hg.at[p, pl.ds(8, 16)], gtb.at[p], 0)
 
     s_id = lax.broadcasted_iota(jnp.int32, (N, N), 0)
     t_id = lax.broadcasted_iota(jnp.int32, (N, N), 1)
@@ -179,21 +159,19 @@
 
     lax.fori_loop(0, HEADS, own_head, 0)
 
-    states = []
-    for r in range(8):
-        arrived(KS, sb.at[r], r)
-        states.append(sb[r].astype(F32))
+    arrived(KS, sb, 0)
+    states = [sb[r].astype(F32) for r in range(8)]
     pair = [states[2 * j] + states[2 * j + 1] for j in range(4)]
     tsend[...] = ((pair[0] + pair[1]) + (pair[2] + pair[3])).astype(BF16)
-    for i, r in enumerate(far):
-        send(KU, i, tsend.at[rows16(r), :], urecv.at[a, 0], a, dev_a(r))
-    local(KU, tsend.at[rows16(a), :], urecv.at[a, 0], a)
-
+    for r in far:
+        send(KU, tsend.at[rows16(r), :], trecv.at[a], 0, dev_a(r))
+    local(KU, tsend.at[rows16(a), :], trecv.at[a], 0)
+
+    arrived(KT, gtb, 0)
     for part in range(2):
         for i, r in enumerate([p] + near):
             if part == 0:
                 arrived(KG, gb.at[r], r)
-                arrived(KT, gtb.at[r], r)
             arrived((KQ, KH)[part], qb.at[r, half[part]], r)
             qt = qb[r, part * 64 : part * 64 + 64].astype(F32)
             rows = gtb[r]
@@ -205,53 +183,44 @@
                 lacc[...] += prod
             else:
                 lbuf[:, part * 64 : part * 64 + 64] = (lacc[...] + prod).astype(BF16).reshape(6, 64, N)
-        for l in range(8, 2, -1):
-            @pl.when(flag[l] == 1)
-            def _():
-                for dz in (2, 1, 3):
-                    r = part * 4 + (zz + dz) % 4
-                    send(KL + l - 3, part * 4 + dz, lbuf.at[l - 3, rows16(r), :], urecv.at[a, l - 2], a, dev_a(r), [])
-                @pl.when(core == part)
-                def _():
-                    local(KL + l - 3, lbuf.at[l - 3, rows16(a), :], urecv.at[a, l - 2], a)
-                @pl.when(core != part)
-                def _():
-                    r = part * 4 + zz
-                    send(KL + l - 3, part * 4, lbuf.at[l - 3, rows16(r), :], urecv.at[a, l - 2], a, dev_a(r), [])
-    kept = {}
+        for dz in (2, 1, 3):
+            r = part * 4 + (zz + dz) % 4
+            send(KL, lbuf.at[:, rows16(r), :], lrecv.at[a], 0, dev_a(r))
+        @pl.when(core == part)
+        def _():
+            local(KL, lbuf.at[:, rows16(a), :], lrecv.at[a], 0)
+        @pl.when(core != part)
+        def _():
+            r = part * 4 + zz
+            send(KL, lbuf.at[:, rows16(r), :], lrecv.at[a], 0, dev_a(r))
+    seven = pl.ds(0, 7)
+    sent(KS, sb.at[seven])
+    sent(KG, gb.at[seven])
+    sent(KT, gtb.at[seven])
+    sent(KQ, qb.at[seven, half[0]])
+    sent(KH, qb.at[seven, half[1]])
 
     ysum[...] = jnp.zeros((4, 16, N), F32)
-    tops = []
-    for r in range(8):
-        arrived(KU, urecv.at[r, 0], r)
-        tops.append(urecv[r, 0].astype(F32))
+    arrived(KU, trecv, 0)
+    tops = [trecv[r].astype(F32) for r in range(8)]
     tpair = [tops[2 * j] + tops[2 * j + 1] for j in range(4)]
     tquad = [tpair[0] + tpair[1], tpair[2] + tpair[3]]
     bsend[0] = tquad[0] + tquad[1]
-    up = []
+    for r in range(7, 0, -1):
+        @pl.when(r > y)
+        def _():
+            send(KB, bsend.at[0], brecv.at[y], y, dev_y(r))
+    none = jnp.zeros((16, N), BF16)
     for r in range(8):
-        up.append([])
-        @pl.when(r > y)
-        def _():
-            send(KB, r, bsend.at[0], brecv.at[y], y, dev_y(r), up[r])
-    for r in range(8):
-        if r & 1:
-            vsend[r, 0] = tops[r - 1].astype(BF16)
-        if r & 2:
-            vsend[r, 1] = tpair[(r >> 1) ^ 1].astype(BF16)
-        if r & 4:
-            vsend[r, 2] = tquad[0].astype(BF16)
-    side = {}
-    for i, r in enumerate(far):
-        for l in range(3):
-            side[i, l] = []
-            @pl.when(r // 2**l % 2 == 1)
-            def _():
-                send(KV + l, i, vsend.at[r, l], rbuf.at[l, rows16(a), :], a, dev_a(r), side[i, l])
-    for l in range(3):
-        @pl.when(flag[3 + l] == 1)
-        def _():
-            local(KV + l, vsend.at[a, l], rbuf.at[l, rows16(a), :], a)
+        vsend[r, 0] = tops[r - 1].astype(BF16) if r & 1 else none
+        vsend[r, 1] = tpair[(r >> 1) ^ 1].astype(BF16) if r & 2 else none
+        vsend[r, 2] = tquad[0].astype(BF16) if r & 4 else none
+    mine = rows16(a)
+    three = pl.ds(0, 3)
+    for r in far:
+        send(KV, vsend.at[r], rbuf.at[three, mine, :], 0, dev_a(r))
+    local(KV, vsend.at[a], rbuf.at[three, mine, :], 0)
+    sent(KU, trecv.at[seven])
 
     low = {}
     for r in range(1, 8):
@@ -292,35 +261,28 @@
             ysum[high] += brecv[r]
     for l in range(3):
         xsend[l] = ysum[l].astype(BF16)
-    for l in range(3):
-        kept[9 + l] = []
-        @pl.when(flag[6 + l] == 1)
-        def _():
-            for i, r in enumerate(far):
-                send(KX + l, i, xsend.at[l], rbuf.at[3 + l, rows16(a), :], a, dev_a(r), kept[9 + l])
-            local(KX + l, xsend.at[l], rbuf.at[3 + l, rows16(a), :], a)
-
+    for r in far:
+        send(KX, xsend, rbuf.at[pl.ds(3, 3), mine, :], 0, dev_a(r))
+    local(KX, xsend, rbuf.at[pl.ds(3, 3), mine, :], 0)
+
+    arrived(KL, lrecv, 0)
+    for l in range(6, 9):
+        total = lrecv[0, l - 3].astype(F32)
+        for r in range(1, 8):
+            total = total + lrecv[r, l - 3].astype(F32)
+        bsend[l - 5] = total
+    for r in range(7):
+        @pl.when(r < y)
+        def _():
+            high = jnp.where(y // 4 != r // 4, 3, jnp.where(y // 2 != r // 2, 2, 1))
+            send(KB, bsend.at[high], brecv.at[y], y, dev_y(r))
     lows = {}
     for l in range(3, 6):
         for r in range(8):
             if r >> (l - 3) & 1:
-                arrived(KL + l - 3, urecv.at[r, l - 2], r)
-                lows[l, r] = urecv[r, l - 2].astype(F32)
-    for l in range(6, 9):
-        @pl.when(flag[l] == 1)
-        def _():
-            total = zero
-            for r in range(8):
-                arrived(KL + l - 3, urecv.at[r, l - 2], r)
-                total = total + urecv[r, l - 2].astype(F32)
-            bsend[l - 5] = total
-    down = []
-    for r in range(8):
-        down.append([])
-        @pl.when(r < y)
-        def _():
-            high = jnp.where(y // 4 != r // 4, 3, jnp.where(y // 2 != r // 2, 2, 1))
-            send(KB, r, bsend.at[high], brecv.at[y], y, dev_y(r), down[r])
+                lows[l, r] = lrecv[r, l - 3].astype(F32)
+    sent(KL, lrecv.at[seven])
+    sent(KV, vsend.at[seven])
     l4 = {3: lows[4, 2] + lows[4, 3], 7: lows[4, 6] + lows[4, 7]}
     l5 = (lows[5, 4] + lows[5, 5]) + (lows[5, 6] + lows[5, 7])
     dmid = []
@@ -334,11 +296,7 @@
             acc = acc + l5
         dmid.append(acc)
 
-    for l in range(3):
-        @pl.when(flag[3 + l] == 1)
-        def _():
-            for r in range(8):
-                arrived(KV + l, rbuf.at[l, pl.ds(16 * r, 16), :], r)
+    arrived(KV, rbuf.at[three], 0)
 
     def middle(b, _):
         rows = gtb[b]
@@ -359,16 +317,13 @@
     dtop = ysum[3]
     for r in range(8):
         wsend[r] = (dmid[r] + dtop).astype(BF16)
-    for i, r in enumerate(far):
-        send(KW, i, wsend.at[r], rbuf.at[6, rows16(a), :], a, dev_a(r))
-    local(KW, wsend.at[a], rbuf.at[6, rows16(a), :], a)
-
-    for l in range(3):
-        @pl.when(flag[6 + l] == 1)
-        def _():
-            for r in range(8):
-                arrived(KX + l, rbuf.at[3 + l, pl.ds(16 * r, 16), :], r)
-
+    for r in far:
+        send(KW, wsend.at[r], rbuf.at[6, mine, :], 0, dev_a(r))
+    local(KW, wsend.at[a], rbuf.at[6, mine, :], 0)
+    sent(KB, brecv.at[seven])
+    sent(KX, rbuf.at[pl.ds(0, 3), pl.ds(0, 112), :])
+
+    arrived(KX, rbuf.at[pl.ds(3, 3)], 0)
     for i, b in enumerate(near + [p]):
         rows = gtb[b]
         prod = nt(rbuf[3:6].reshape(3 * N, N), gb[b])
@@ -377,15 +332,15 @@
             acc = acc + rows[6 + l : 7 + l, :] * prod[l * N : (l + 1) * N]
         csend[b] = acc.T.astype(BF16)
         if i < 7:
-            send(KC, i, csend.at[b], crecv.at[p], p, dev_p(b))
+            send(KC, csend.at[b], crecv.at[p], p, dev_p(b))
     local(KC, csend.at[p], crecv.at[p], p)
 
-    for r in range(8):
-        arrived(KW, rbuf.at[6, pl.ds(16 * r, 16), :], r)
+    sent(KW, wsend.at[seven])
+    arrived(KW, rbuf.at[6], 0)
     dall = rbuf[6].astype(F32)
-    for i, r in enumerate(near):
+    for r in near:
         dsend[r] = (dacc[r] + dall).astype(BF16)
-        send(KD, i, dsend.at[r], drecv.at[p], p, dev_p(r))
+        send(KD, dsend.at[r], drecv.at[p], p, dev_p(r))
     dsend[p] = (dacc[p] + dall).astype(BF16)
     local(KD, dsend.at[p], drecv.at[p], p)
 
@@ -393,6 +348,7 @@
         c = pl.ds(pl.multiple_of(r * N, N), N)
         arrived(KC, crecv.at[r], r)
         qo_ref[:, c] = (qloc[:, c] + crecv[r].astype(F32)).astype(BF16)
+    sent(KC, csend.at[seven])
     for r in [p] + near:
         c = pl.ds(pl.multiple_of(r * N, N), N)
         arrived(KD, drecv.at[r], r)
@@ -400,31 +356,7 @@
         ko_ref[:, c] = (kloc[:, c] + nt(v_ref[:, c], d)).astype(BF16)
         vo_ref[:, c] = (vloc[:, c] + nn(k_ref[:, c], d)).astype(BF16)
 
-    sent(sends)
-    for part in range(2):
-        for l in range(3, 9):
-            @pl.when(flag[l] == 1)
-            def _():
-                sent([(KL + l - 3, part * 4 + dz) for dz in (1, 2, 3)])
-                @pl.when(core != part)
-                def _():
-                    sent([(KL + l - 3, part * 4)])
-    for l in range(9, 12):
-        @pl.when(flag[l if l < 9 else l - 3] == 1)
-        def _():
-            sent(kept[l])
-    for r in range(8):
-        @pl.when(r < y)
-        def _():
-            sent(down[r])
-        @pl.when(r > y)
-        def _():
-            sent(up[r])
-    for i, r in enumerate(far):
-        for l in range(3):
-            @pl.when(r // 2**l % 2 == 1)
-            def _():
-                sent(side[i, l])
+    sent(KD, dsend.at[seven])
 
 
 def write_out(qi, ki, vi, qo, ko, vo, sem):
@@ -461,7 +393,8 @@
             wide, wide, wide,
             pltpu.VMEM((N, N), BF16),
             cube(6, BF16),
-            pltpu.VMEM((8, 7, 16, N), BF16),
+            pltpu.VMEM((8, 16, N), BF16),
+            pltpu.VMEM((8, 6, 16, N), BF16),
             pltpu.VMEM((4, 16, N), F32),
             pltpu.VMEM((8, 16, N), F32),
             pltpu.VMEM((4, 16, N), F32),
@@ -472,7 +405,7 @@
             cube(8, F32), cube(8, F32),
             cube(8, BF16), cube(8, BF16), cube(8, BF16), cube(8, BF16),
             pltpu.SemaphoreType.DMA((6,)),
-            pltpu.SemaphoreType.DMA((KINDS, 8)),
+            pltpu.SemaphoreType.DMA((KINDS,)),
             pltpu.SemaphoreType.DMA((KINDS, 8)),
         ],
         compiler_params=pltpu.CompilerParams(

time: 53.7 us -> 53.4 us (level)
  no operation moved by 1% of the time
where the time goes in v5:
time: 53.4 us; the launch traced here: 53.2 us
  Pallas kernels  52.6 us (99%)
  between operations  0.64 us (1%)
    pallas_call x1, Pallas kernels, per_device(): pl.pallas_call(kernel, out_shape=(out, out, out), in_specs=[hbm] * 6, out...  51.7 us

profile of v5, /device:TPU:1, one launch (start us, length us, event | category | flops | bytes accessed | tf_op | source)
XLA Modules:
  0.0 53.2 jit_solution(1798510863641775914)
XLA Ops:
  0.6 51.7 %shard_map.85 = (bf16[128,1024]{1,0:T(8,128)(2,1)S(1)}, bf16[128,1024]{1,0:T(8,128)(2,1)S(1)}, bf16[128,1024]{1,0:T(8,128)(2,1)S(1)}) custom-call(bf16[128,1024]{1,0:T(8,128)(2,1)} %q_hbm.1, bf16[128,1024]{1,0:T(8,128)(2,1)} %k_hbm.1, bf16[128,1024]{1,0:T(8,128)(2,1)} %v_hbm.1, bf16[128,1024]{1,0:T(8,128)(2,1)} %g_hbm.1, s32[1,128]{1,0:T(1,128)} %bitcast.3, ...), custom_call_target="tpu_custom_call" | custom-call | tf_op jit(solution)/shard_map/pallas_call | solution.py:378
  52.3 0.9 %shard_map.86 = (bf16[128,1024]{1,0:T(8,128)(2,1)}, bf16[128,1024]{1,0:T(8,128)(2,1)}, bf16[128,1024]{1,0:T(8,128)(2,1)}) custom-call(bf16[128,1024]{1,0:T(8,128)(2,1)S(1)} %get-tuple-element.6.qi, bf16[128,1024]{1,0:T(8,128)(2,1)S(1)} %get-tuple-element.7.ki, bf16[128,1024]{1,0:T(8,128)(2,1)S(1)} %get-tuple-element.8.vi), custom_call_target="tpu_custom_call" | custom-call | tf_op jit(solution)/shard_map/pallas_call | solution.py:415

commit v6 on v5

--- a/solution.py
+++ b/solution.py
@@ -10,9 +10,9 @@
 BF16 = jnp.bfloat16
 N = 128
 HEADS = 8
-KS, KG, KT, KQ, KH, KU, KL, KB, KV, KX, KW, KC, KD = range(13)
-KINDS = 13
-NEAR = ((0, 1), (0, 3), (1, 0), (1, 1), (1, 3), (0, 2), (1, 2))
+KS, KG, KT, KQ, KH, KU, KL, KB, KV, KX, KW, KC, KD, KM = range(14)
+KINDS = 14
+NEAR = ((1, 2), (0, 2), (1, 1), (1, 3), (1, 0), (0, 1), (0, 3))
 FAR = ((0, 2), (1, 2), (0, 1), (0, 3), (1, 1), (1, 3), (1, 0))
 
 
@@ -62,8 +62,8 @@
         return (r * 2 + core, gy)
 
     barrier = pltpu.get_barrier_semaphore()
-    for i in range(7):
-        for dev in (dev_p(near[i]), dev_a(far[i]), dev_y((y + i + 1) % 8)):
+    for i, dy in enumerate((4, 3, 5, 2, 6, 1, 7)):
+        for dev in (dev_a(far[i]), dev_y((y + dy) % 8), dev_p(near[i])):
             pl.semaphore_signal(barrier, inc=1, device_id=dev, device_id_type=MESH)
 
     loads = []
@@ -123,10 +123,12 @@
     for r in near:
         send(KG, cols(g_ref, r), gb.at[p], p, dev_p(r))
         send(KT, hg.at[r, pl.ds(8, 16)], gtb.at[p], 0, dev_p(r))
-    for kind, part in ((KQ, half[0]), (KH, half[1])):
-        for r in near:
-            send(kind, qt_send.at[r, part], qb.at[p, part], p, dev_p(r))
-        local(kind, qt_send.at[p, part], qb.at[p, part], p)
+    for r in near:
+        send(KQ, qt_send.at[r, half[0]], qb.at[p, half[0]], p, dev_p(r))
+    for r in near:
+        send(KH, qt_send.at[r, half[1]], qb.at[p, half[1]], p, dev_p(r))
+    local(KQ, qt_send.at[p, half[0]], qb.at[p, half[0]], p)
+    local(KH, qt_send.at[p, half[1]], qb.at[p, half[1]], p)
     local(KS, st_send.at[p], sb.at[p], 0)
     local(KG, cols(g_ref, p), gb.at[p], p)
     local(KT, hg.at[p, pl.ds(8, 16)], gtb.at[p], 0)
@@ -159,6 +161,8 @@
 
     lax.fori_loop(0, HEADS, own_head, 0)
 
+    mine = rows16(a)
+    three = pl.ds(0, 3)
     arrived(KS, sb, 0)
     states = [sb[r].astype(F32) for r in range(8)]
     pair = [states[2 * j] + states[2 * j + 1] for j in range(4)]
@@ -168,7 +172,7 @@
     local(KU, tsend.at[rows16(a), :], trecv.at[a], 0)
 
     arrived(KT, gtb, 0)
-    for part in range(2):
+    def raise_half(part):
         for i, r in enumerate([p] + near):
             if part == 0:
                 arrived(KG, gb.at[r], r)
@@ -183,16 +187,21 @@
                 lacc[...] += prod
             else:
                 lbuf[:, part * 64 : part * 64 + 64] = (lacc[...] + prod).astype(BF16).reshape(6, 64, N)
-        for dz in (2, 1, 3):
-            r = part * 4 + (zz + dz) % 4
-            send(KL, lbuf.at[:, rows16(r), :], lrecv.at[a], 0, dev_a(r))
-        @pl.when(core == part)
-        def _():
-            local(KL, lbuf.at[:, rows16(a), :], lrecv.at[a], 0)
-        @pl.when(core != part)
-        def _():
-            r = part * 4 + zz
-            send(KL, lbuf.at[:, rows16(r), :], lrecv.at[a], 0, dev_a(r))
+        for kind, levels in ((KL, pl.ds(3, 3)), (KM, pl.ds(0, 3))):
+            for dz in (2, 1, 3):
+                r = part * 4 + (zz + dz) % 4
+                send(kind, lbuf.at[levels, rows16(r), :], lrecv.at[a, levels], 0, dev_a(r))
+            @pl.when(core == part)
+            def _():
+                local(kind, lbuf.at[levels, rows16(a), :], lrecv.at[a, levels], 0)
+            @pl.when(core != part)
+            def _():
+                r = part * 4 + zz
+                send(kind, lbuf.at[levels, rows16(r), :], lrecv.at[a, levels], 0, dev_a(r))
+
+    raise_half(0)
+    raise_half(1)
+
     seven = pl.ds(0, 7)
     sent(KS, sb.at[seven])
     sent(KG, gb.at[seven])
@@ -210,16 +219,6 @@
         @pl.when(r > y)
         def _():
             send(KB, bsend.at[0], brecv.at[y], y, dev_y(r))
-    none = jnp.zeros((16, N), BF16)
-    for r in range(8):
-        vsend[r, 0] = tops[r - 1].astype(BF16) if r & 1 else none
-        vsend[r, 1] = tpair[(r >> 1) ^ 1].astype(BF16) if r & 2 else none
-        vsend[r, 2] = tquad[0].astype(BF16) if r & 4 else none
-    mine = rows16(a)
-    three = pl.ds(0, 3)
-    for r in far:
-        send(KV, vsend.at[r], rbuf.at[three, mine, :], 0, dev_a(r))
-    local(KV, vsend.at[a], rbuf.at[three, mine, :], 0)
     sent(KU, trecv.at[seven])
 
     low = {}
@@ -253,19 +252,7 @@
                 acc = acc + rows[l : l + 1, :] * nt(left, gb[b])
         ctr[b] = acc
 
-    for r in range(7):
-        @pl.when(r < y)
-        def _():
-            arrived(KB, brecv.at[r], r)
-            high = jnp.where(y // 4 != r // 4, 2, jnp.where(y // 2 != r // 2, 1, 0))
-            ysum[high] += brecv[r]
-    for l in range(3):
-        xsend[l] = ysum[l].astype(BF16)
-    for r in far:
-        send(KX, xsend, rbuf.at[pl.ds(3, 3), mine, :], 0, dev_a(r))
-    local(KX, xsend, rbuf.at[pl.ds(3, 3), mine, :], 0)
-
-    arrived(KL, lrecv, 0)
+    arrived(KL, lrecv.at[:, pl.ds(3, 3)], 0)
     for l in range(6, 9):
         total = lrecv[0, l - 3].astype(F32)
         for r in range(1, 8):
@@ -276,13 +263,14 @@
         def _():
             high = jnp.where(y // 4 != r // 4, 3, jnp.where(y // 2 != r // 2, 2, 1))
             send(KB, bsend.at[high], brecv.at[y], y, dev_y(r))
+    arrived(KM, lrecv.at[:, pl.ds(0, 3)], 0)
     lows = {}
     for l in range(3, 6):
         for r in range(8):
             if r >> (l - 3) & 1:
                 lows[l, r] = lrecv[r, l - 3].astype(F32)
-    sent(KL, lrecv.at[seven])
-    sent(KV, vsend.at[seven])
+    sent(KL, lrecv.at[seven, pl.ds(0, 3)])
+    sent(KM, lrecv.at[seven, pl.ds(0, 3)])
     l4 = {3: lows[4, 2] + lows[4, 3], 7: lows[4, 6] + lows[4, 7]}
     l5 = (lows[5, 4] + lows[5, 5]) + (lows[5, 6] + lows[5, 7])
     dmid = []
@@ -296,6 +284,26 @@
             acc = acc + l5
         dmid.append(acc)
 
+    none = jnp.zeros((16, N), BF16)
+    for r in range(8):
+        vsend[r, 0] = tops[r - 1].astype(BF16) if r & 1 else none
+        vsend[r, 1] = tpair[(r >> 1) ^ 1].astype(BF16) if r & 2 else none
+        vsend[r, 2] = tquad[0].astype(BF16) if r & 4 else none
+    for r in far:
+        send(KV, vsend.at[r], rbuf.at[three, mine, :], 0, dev_a(r))
+    local(KV, vsend.at[a], rbuf.at[three, mine, :], 0)
+    for r in range(7):
+        @pl.when(r < y)
+        def _():
+            arrived(KB, brecv.at[r], r)
+            high = jnp.where(y // 4 != r // 4, 2, jnp.where(y // 2 != r // 2, 1, 0))
+            ysum[high] += brecv[r]
+    for l in range(3):
+        xsend[l] = ysum[l].astype(BF16)
+    for r in far:
+        send(KX, xsend, rbuf.at[pl.ds(3, 3), mine, :], 0, dev_a(r))
+    local(KX, xsend, rbuf.at[pl.ds(3, 3), mine, :], 0)
+
     arrived(KV, rbuf.at[three], 0)
 
     def middle(b, _):
@@ -320,9 +328,10 @@
     for r in far:
         send(KW, wsend.at[r], rbuf.at[6, mine, :], 0, dev_a(r))
     local(KW, wsend.at[a], rbuf.at[6, mine, :], 0)
+
+    sent(KV, vsend.at[seven])
     sent(KB, brecv.at[seven])
     sent(KX, rbuf.at[pl.ds(0, 3), pl.ds(0, 112), :])
-
     arrived(KX, rbuf.at[pl.ds(3, 3)], 0)
     for i, b in enumerate(near + [p]):
         rows = gtb[b]
@@ -348,7 +357,6 @@
         c = pl.ds(pl.multiple_of(r * N, N), N)
         arrived(KC, crecv.at[r], r)
         qo_ref[:, c] = (qloc[:, c] + crecv[r].astype(F32)).astype(BF16)
-    sent(KC, csend.at[seven])
     for r in [p] + near:
         c = pl.ds(pl.multiple_of(r * N, N), N)
         arrived(KD, drecv.at[r], r)
@@ -356,11 +364,16 @@
         ko_ref[:, c] = (kloc[:, c] + nt(v_ref[:, c], d)).astype(BF16)
         vo_ref[:, c] = (vloc[:, c] + nn(k_ref[:, c], d)).astype(BF16)
 
+    sent(KC, csend.at[seven])
     sent(KD, dsend.at[seven])
 
 
 def write_out(qi, ki, vi, qo, ko, vo, sem):
-    copies = [pltpu.make_async_copy(s, d, sem.at[i]) for i, (s, d) in enumerate(((qi, qo), (ki, ko), (vi, vo)))]
+    copies = []
+    for i, (src, dst) in enumerate(((qi, qo), (ki, ko), (vi, vo))):
+        for j in range(2):
+            rows = pl.ds(j * (N // 2), N // 2)
+            copies.append(pltpu.make_async_copy(src.at[rows], dst.at[rows], sem.at[2 * i + j]))
     for copy in copies:
         copy.start()
     for copy in copies:
@@ -418,7 +431,7 @@
         in_specs=[vmem] * 3,
         out_specs=(hbm, hbm, hbm),
         compiler_params=pltpu.CompilerParams(vmem_limit_bytes=16 * 1024 * 1024),
-        scratch_shapes=[pltpu.SemaphoreType.DMA((3,))],
+        scratch_shapes=[pltpu.SemaphoreType.DMA((6,))],
     )(*outs)
 
 

time: 53.4 us -> 52.5 us (0.983)
  Pallas kernels: 52.6 us -> 51.7 us
    pallas_call x1, Pallas kernels: 51.7 us -> 50.8 us  [per_device(): pl.pallas_call(kernel, out_shape=(out, out, out), in_specs=[hbm] * 6, out...]
where the time goes in v6:
time: 52.5 us; the launch traced here: 52.3 us
  Pallas kernels  51.7 us (98%)
  between operations  0.64 us (1%)
    pallas_call x1, Pallas kernels, per_device(): pl.pallas_call(kernel, out_shape=(out, out, out), in_specs=[hbm] * 6, out...  50.8 us

profile of v6, /device:TPU:1, one launch (start us, length us, event | category | flops | bytes accessed | tf_op | source)
XLA Modules:
  0.0 52.3 jit_solution(15478471150680093498)
XLA Ops:
  0.6 50.8 %shard_map.85 = (bf16[128,1024]{1,0:T(8,128)(2,1)S(1)}, bf16[128,1024]{1,0:T(8,128)(2,1)S(1)}, bf16[128,1024]{1,0:T(8,128)(2,1)S(1)}) custom-call(bf16[128,1024]{1,0:T(8,128)(2,1)} %q_hbm.1, bf16[128,1024]{1,0:T(8,128)(2,1)} %k_hbm.1, bf16[128,1024]{1,0:T(8,128)(2,1)} %v_hbm.1, bf16[128,1024]{1,0:T(8,128)(2,1)} %g_hbm.1, s32[1,128]{1,0:T(1,128)} %bitcast.3, ...), custom_call_target="tpu_custom_call" | custom-call | tf_op jit(solution)/shard_map/pallas_call | solution.py:391
  51.4 0.9 %shard_map.86 = (bf16[128,1024]{1,0:T(8,128)(2,1)}, bf16[128,1024]{1,0:T(8,128)(2,1)}, bf16[128,1024]{1,0:T(8,128)(2,1)}) custom-call(bf16[128,1024]{1,0:T(8,128)(2,1)S(1)} %get-tuple-element.6.qi, bf16[128,1024]{1,0:T(8,128)(2,1)S(1)} %get-tuple-element.7.ki, bf16[128,1024]{1,0:T(8,128)(2,1)S(1)} %get-tuple-element.8.vi), custom_call_target="tpu_custom_call" | custom-call | tf_op jit(solution)/shard_map/pallas_call | solution.py:428

commit v7 on v6

--- a/solution.py
+++ b/solution.py
@@ -94,6 +94,11 @@
     def rows16(r):
         return pl.ds(pl.multiple_of(r * 16, 16), 16)
 
+    loads[3].wait()
+    pl.semaphore_wait(barrier, 21)
+    for r in near:
+        send(KG, cols(g_ref, r), gb.at[p], p, dev_p(r))
+
     zero = jnp.zeros((16, N), F32)
     loads[0].wait()
     loads[1].wait()
@@ -113,15 +118,11 @@
         c = slice(h * N, h * N + N)
         st_send[h] = tn(k_ref[:, c], v_ref[:, c]).astype(BF16)
         qt_send[h] = q_ref[:, c].T
-    loads[3].wait()
-
-    pl.semaphore_wait(barrier, 21)
 
     half = (pl.ds(0, 64), pl.ds(64, 64))
     for r in near:
         send(KS, st_send.at[r], sb.at[p], 0, dev_p(r))
     for r in near:
-        send(KG, cols(g_ref, r), gb.at[p], p, dev_p(r))
         send(KT, hg.at[r, pl.ds(8, 16)], gtb.at[p], 0, dev_p(r))
     for r in near:
         send(KQ, qt_send.at[r, half[0]], qb.at[p, half[0]], p, dev_p(r))

time: 52.5 us -> 52.2 us (level)
  no operation moved by 1% of the time
where the time goes in v7:
time: 52.2 us; the launch traced here: 52 us
  Pallas kernels  51.4 us (98%)
  between operations  0.64 us (1%)
    pallas_call x1, Pallas kernels, per_device(): pl.pallas_call(kernel, out_shape=(out, out, out), in_specs=[hbm] * 6, out...  50.4 us

profile of v7, /device:TPU:1, one launch (start us, length us, event | category | flops | bytes accessed | tf_op | source)
XLA Modules:
  0.0 52.0 jit_solution(4696103390724342933)
XLA Ops:
  0.6 50.4 %shard_map.85 = (bf16[128,1024]{1,0:T(8,128)(2,1)S(1)}, bf16[128,1024]{1,0:T(8,128)(2,1)S(1)}, bf16[128,1024]{1,0:T(8,128)(2,1)S(1)}) custom-call(bf16[128,1024]{1,0:T(8,128)(2,1)} %q_hbm.1, bf16[128,1024]{1,0:T(8,128)(2,1)} %k_hbm.1, bf16[128,1024]{1,0:T(8,128)(2,1)} %v_hbm.1, bf16[128,1024]{1,0:T(8,128)(2,1)} %g_hbm.1, s32[1,128]{1,0:T(1,128)} %bitcast.3, ...), custom_call_target="tpu_custom_call" | custom-call | tf_op jit(solution)/shard_map/pallas_call | solution.py:392
  51.1 0.9 %shard_map.86 = (bf16[128,1024]{1,0:T(8,128)(2,1)}, bf16[128,1024]{1,0:T(8,128)(2,1)}, bf16[128,1024]{1,0:T(8,128)(2,1)}) custom-call(bf16[128,1024]{1,0:T(8,128)(2,1)S(1)} %get-tuple-element.6.qi, bf16[128,1024]{1,0:T(8,128)(2,1)S(1)} %get-tuple-element.7.ki, bf16[128,1024]{1,0:T(8,128)(2,1)S(1)} %get-tuple-element.8.vi), custom_call_target="tpu_custom_call" | custom-call | tf_op jit(solution)/shard_map/pallas_call | solution.py:429
